TPU v7x, 128 devices: a whole 4x4x4 slice. The times are simulated.
128 devices in a mesh: grp: 16 (over z, x), loc: 8 (over y, core).
Axes of the slice: x: 4, y: 4, z: 4, core: 2. Of those that a mesh axis runs over, the one named last changes fastest.
Arguments:
- acts: bfloat16 [16384, 2048], P(('grp', 'loc')), may hold values from -6 to 6
- out_grad: bfloat16 [16384, 2048], P(('grp', 'loc')), may hold values from -6 to 6
- expert_ids: int32 [16384, 8], P(('grp', 'loc')), may hold values from 0 to 127, all different within a row; in each aligned block of 128 rows (0 to 127, 128 to 255, ...) at most 9 rows name the same one
- gate_vals: bfloat16 [16384, 8], P(('grp', 'loc')), may hold values from 0.049804688 to 0.5
- w_gate: bfloat16 [128, 2048, 768], P(('grp', 'loc')), may hold values from -0.125 to 0.125
- w_up: bfloat16 [128, 2048, 768], P(('grp', 'loc')), may hold values from -0.125 to 0.125
- w_down: bfloat16 [128, 768, 2048], P(('grp', 'loc')), may hold values from -0.21875 to 0.21875
Outputs:
- grad_acts: bfloat16 [16384, 2048], P(('grp', 'loc'))
- grad_gates: bfloat16 [16384, 8], P(('grp', 'loc'))
- grad_w_gate: bfloat16 [128, 2048, 768], P(('grp', 'loc'))
- grad_w_up: bfloat16 [128, 2048, 768], P(('grp', 'loc'))
- grad_w_down: bfloat16 [128, 768, 2048], P(('grp', 'loc'))
Inputs may be any that keep to these rules, and one draw needn't show every extreme that they name: `expert_ids`: each token names 8 different experts. Among the 128 tokens of one device, no expert is named by more than 9 of them, and in every draw some expert is named by exactly 9 of one device's tokens.
All inputs are finite; a program needn't handle non-finite values.
Results may differ from a plain program's by a relative error of at most 0.0058.
Values may be sent and summed in bfloat16 or wider, within the bound.
No kernel may reach another device: no remote copies, remote signals or barrier semaphores. Data moves between devices by JAX's collectives and lax.ppermute only.
A program may use at most 128 MiB of HBM per device.

v0:
```python
import jax
import jax.numpy as jnp
from jax import lax
from jax.sharding import PartitionSpec as P


def contract(left, right, left_dim, right_dim):
    return lax.dot_general(
        left, right, (((left_dim,), (right_dim,)), ((), ())), preferred_element_type=jnp.float32
    )


def expert_grads(rows_in, rows_grad, rows_gate, wg_one, wu_one, wd_one):
    gate_pre = jnp.dot(rows_in, wg_one, preferred_element_type=jnp.float32)
    up_proj = jnp.dot(rows_in, wu_one, preferred_element_type=jnp.float32)
    sigmoid_gate = jax.nn.sigmoid(gate_pre)
    activated = gate_pre * sigmoid_gate
    hidden = activated * up_proj
    dh_raw = contract(rows_grad, wd_one, 1, 1)
    gate_grad = jnp.sum(hidden * dh_raw, axis=1).astype(jnp.bfloat16)
    weight_col = rows_gate.astype(jnp.float32)[:, None]
    scaled_hidden = (weight_col * hidden).astype(jnp.bfloat16)
    down_grad = contract(scaled_hidden, rows_grad, 0, 0).astype(jnp.bfloat16)
    hidden_grad = weight_col * dh_raw
    pre_grad = (
        hidden_grad * up_proj * sigmoid_gate * (1.0 + gate_pre * (1.0 - sigmoid_gate))
    ).astype(jnp.bfloat16)
    up_grad = (hidden_grad * activated).astype(jnp.bfloat16)
    wg_grad = contract(rows_in, pre_grad, 0, 0).astype(jnp.bfloat16)
    wu_grad = contract(rows_in, up_grad, 0, 0).astype(jnp.bfloat16)
    input_grad = (contract(pre_grad, wg_one, 1, 1) + contract(up_grad, wu_one, 1, 1)).astype(
        jnp.bfloat16
    )
    return (input_grad, gate_grad, wg_grad, wu_grad, down_grad)


def body(acts, out_grad, expert_ids, gate_vals, w_gate, w_up, w_down):
    tokens = acts.shape[0]
    width = acts.shape[1]
    top_count = expert_ids.shape[1]
    n_group = lax.axis_size("grp")
    n_local = lax.axis_size("loc")
    experts = n_group * n_local
    capacity = 9 * tokens * top_count // (8 * experts)
    slot_count = experts * capacity
    entries = tokens * top_count
    flat_ids = expert_ids.reshape(-1)
    one_hot = (flat_ids[:, None] == jnp.arange(experts, dtype=jnp.int32)[None, :]).astype(jnp.int32)
    before = jnp.cumsum(one_hot, axis=0) - one_hot
    rank_in = jnp.sum(before * one_hot, axis=1)
    slot_of = flat_ids * capacity + rank_in
    source = (
        jnp.full((slot_count,), entries, jnp.int32)
        .at[slot_of]
        .set(jnp.arange(entries, dtype=jnp.int32))
    )
    row_of = source // top_count
    padded_acts = jnp.concatenate([acts, jnp.zeros((1, width), acts.dtype)], axis=0)
    padded_grad = jnp.concatenate([out_grad, jnp.zeros((1, width), out_grad.dtype)], axis=0)
    padded_gate = jnp.concatenate([gate_vals.reshape(-1), jnp.zeros((1,), gate_vals.dtype)], axis=0)
    send_acts = padded_acts[row_of]
    send_grad = padded_grad[row_of]
    send_gate = padded_gate[source]
    recv_acts, recv_grad, recv_gate = (
        lax.all_to_all(send_acts, ("grp", "loc"), split_axis=0, concat_axis=0, tiled=True),
        lax.all_to_all(send_grad, ("grp", "loc"), split_axis=0, concat_axis=0, tiled=True),
        lax.all_to_all(send_gate, ("grp", "loc"), split_axis=0, concat_axis=0, tiled=True),
    )
    input_grad, gate_grad, wg_grad, wu_grad, down_grad = expert_grads(
        recv_acts, recv_grad, recv_gate, w_gate[0], w_up[0], w_down[0]
    )
    back_rows, back_gate = (
        lax.all_to_all(input_grad, ("grp", "loc"), split_axis=0, concat_axis=0, tiled=True),
        lax.all_to_all(gate_grad, ("grp", "loc"), split_axis=0, concat_axis=0, tiled=True),
    )
    picked = back_rows[slot_of].reshape(tokens, top_count, width).astype(jnp.float32)
    grad_acts = jnp.sum(picked, axis=1).astype(jnp.bfloat16)
    grad_gates = back_gate[slot_of].reshape(tokens, top_count)
    return (grad_acts, grad_gates, wg_grad[None], wu_grad[None], down_grad[None])


def solution(mesh):
    placed = (
        P(("grp", "loc"), None),
        P(("grp", "loc"), None),
        P(("grp", "loc"), None),
        P(("grp", "loc"), None),
        P(("grp", "loc"), None, None),
        P(("grp", "loc"), None, None),
        P(("grp", "loc"), None, None),
    )
    return jax.shard_map(
        body,
        mesh=mesh,
        in_specs=placed,
        out_specs=(
            P(("grp", "loc"), None),
            P(("grp", "loc"), None),
            P(("grp", "loc"), None, None),
            P(("grp", "loc"), None, None),
            P(("grp", "loc"), None, None),
        ),
        check_vma=False,
    )
```

profile of v0, /device:TPU:13, one launch (start us, length us, event | category | flops | bytes accessed | tf_op | source)
XLA Modules:
  0.0 456.7 jit_solution(15741429325362480807)
XLA Ops:
  4.8 1.1 broadcast_add_fusion
  6.4 4.3 scatter_custom_fusion
  10.8 7.3 %gather_fusion = bf16[1152]{0:T(1024)(128)(2,1)S(1)} fusion(bf16[1025]{0:T(1024)(128)(2,1)S(1)} %pad_maximum_fusion, s32[2048]{0:T(1024)S(1)} %get-tuple-element.21), kind=kCustom, calls=%fused_computation | custom fusion | bytes 9216 | tf_op jit(solution)/shard_map/gather | solution.py:63
  18.9 10.7 %all-to-all-start = ((bf16[128,9,1]{1,2,0:T(2,128)(2,1)}), bf16[128,9,1]{1,2,0:T(2,128)(2,1)S(1)}, u32[]{:S(2)}, u32[]{:S(2)}) async-start(bf16[128,9,1]{1,2,0:T(2,128)(2,1)} %all_to_all.49), calls=%async_computation | async-start | bytes 131072 | tf_op jit(solution)/shard_map/all_to_all | solution.py:67
  29.6 1.9 concatenate.11
  31.5 11.8 %gather_fusion.2 = bf16[1152,2048]{1,0:T(8,128)(2,1)} fusion(bf16[129,2048]{1,0:T(8,128)(2,1)} %concatenate.11, s32[2048]{0:T(1024)S(1)} %get-tuple-element.20), kind=kCustom, calls=%fused_computation.2 | custom fusion | bytes 9441792 | tf_op jit(solution)/shard_map/gather | solution.py:61
  43.3 8.1 %all_to_all.41 = bf16[128,9,2048]{2,1,0:T(8,128)(2,1)} reshape(bf16[1152,2048]{1,0:T(8,128)(2,1)} %gather_fusion.2) | data formatting | bytes 9437184 | tf_op jit(solution)/shard_map/all_to_all | solution.py:65
  51.4 10.2 %all-to-all-start.2 = ((bf16[128,9,2048]{2,1,0:T(8,128)(2,1)}), bf16[128,9,2048]{2,1,0:T(8,128)(2,1)}, u32[]{:S(2)}, u32[]{:S(2)}) async-start(bf16[128,9,2048]{2,1,0:T(8,128)(2,1)} %all_to_all.41), calls=%async_computation.2 | async-start | bytes 16777216 | tf_op jit(solution)/shard_map/all_to_all | solution.py:65
  61.6 1.9 concatenate.10
  63.5 11.8 %gather_fusion.1 = bf16[1152,2048]{1,0:T(8,128)(2,1)} fusion(bf16[129,2048]{1,0:T(8,128)(2,1)} %concatenate.10, s32[2048]{0:T(1024)S(1)} %get-tuple-element.20), kind=kCustom, calls=%fused_computation.1 | custom fusion | bytes 9441792 | tf_op jit(solution)/shard_map/gather | solution.py:62
  75.4 8.1 %all_to_all.38 = bf16[128,9,2048]{2,1,0:T(8,128)(2,1)} reshape(bf16[1152,2048]{1,0:T(8,128)(2,1)} %gather_fusion.1) | data formatting | bytes 9437184 | tf_op jit(solution)/shard_map/all_to_all | solution.py:66
  83.4 78.0 %all-to-all-done.2 = bf16[128,9,2048]{2,1,0:T(8,128)(2,1)} async-done(((bf16[128,9,2048]{2,1,0:T(8,128)(2,1)}), bf16[128,9,2048]{2,1,0:T(8,128)(2,1)}, u32[]{:S(2)}, u32[]{:S(2)}) %all-to-all-start.2) | async-done | bytes 4718624 | tf_op jit(solution)/shard_map/all_to_all | solution.py:65
  161.4 9.1 %all-to-all-start.1 = ((bf16[128,9,2048]{2,1,0:T(8,128)(2,1)}), bf16[128,9,2048]{2,1,0:T(8,128)(2,1)}, u32[]{:S(2)}, u32[]{:S(2)}) async-start(bf16[128,9,2048]{2,1,0:T(8,128)(2,1)} %all_to_all.38), calls=%async_computation.1 | async-start | bytes 16777216 | tf_op jit(solution)/shard_map/all_to_all | solution.py:66
  171.0 8.4 %all_to_all.43 = bf16[1152,2048]{1,0:T(8,128)(2,1)} reshape(bf16[128,9,2048]{2,1,0:T(8,128)(2,1)} %all-to-all-done.2) | data formatting | bytes 9437184 | tf_op jit(solution)/shard_map/all_to_all | solution.py:65
  179.4 8.5 %fusion.3 = f32[1152,768]{0,1:T(8,128)} fusion(bf16[1152,2048]{1,0:T(8,128)(2,1)} %all_to_all.43, bf16[1,2048,768]{2,1,0:T(8,128)(2,1)S(1)} %copy-done), kind=kOutput, calls=%fused_computation.19 | convolution fusion | flops 3623878656 | bytes 11403264 | tf_op jit(solution)/shard_map/dot_general | solution.py:14
  188.0 6.3 %fusion.6 = f32[1152,768]{0,1:T(8,128)} fusion(bf16[1152,2048]{1,0:T(8,128)(2,1)S(1)} %copy-done.2, bf16[1,2048,768]{2,1,0:T(8,128)(2,1)S(1)} %copy-done.4), kind=kOutput, calls=%fused_computation.22 | convolution fusion | flops 3623878656 | bytes 11403264 | tf_op jit(solution)/shard_map/dot_general | solution.py:15
  194.3 76.4 %all-to-all-done.1 = bf16[128,9,2048]{2,1,0:T(8,128)(2,1)} async-done(((bf16[128,9,2048]{2,1,0:T(8,128)(2,1)}), bf16[128,9,2048]{2,1,0:T(8,128)(2,1)}, u32[]{:S(2)}, u32[]{:S(2)}) %all-to-all-start.1) | async-done | bytes 4718624 | tf_op jit(solution)/shard_map/all_to_all | solution.py:66
  270.6 8.6 %all_to_all.40 = bf16[1152,2048]{1,0:T(8,128)(2,1)} reshape(bf16[128,9,2048]{2,1,0:T(8,128)(2,1)} %all-to-all-done.1) | data formatting | bytes 9437184 | tf_op jit(solution)/shard_map/all_to_all | solution.py:66
  279.3 12.6 %multiply_reduce_fusion = (bf16[1152]{0:T(1024)(128)(2,1)S(1)}, bf16[1152,768]{0,1:T(8,128)(2,1)}, bf16[1152,768]{0,1:T(8,128)(2,1)}) fusion(f32[1152,768]{0,1:T(8,128)} %fusion.6, f32[1152,768]{0,1:T(8,128)} %fusion.3, f32[1152]{0:T(1024)S(1)} %reshape.97, bf16[1152,2048]{1,0:T(8,128)(2,1)} %all_to_all.40, bf16[1,768,2048]{2,1,0:T(8,128)(2,1)} %param.13), kind=kOutput, calls=%fused_computation.9 | convolution fusion | flops 3638918144 | bytes 18488064 | tf_op jit(solution)/shard_map/dot_general | solution.py:8
  292.8 7.3 %all-to-all-start.4 = ((bf16[128,9,1]{1,2,0:T(2,128)(2,1)}), bf16[128,9,1]{1,2,0:T(2,128)(2,1)S(1)}, u32[]{:S(2)}, u32[]{:S(2)}) async-start(bf16[128,9,1]{1,2,0:T(2,128)(2,1)} %convert_element_type.67), calls=%async_computation.4 | async-start | bytes 131072 | tf_op jit(solution)/shard_map/all_to_all | solution.py:74
  300.2 5.6 %fusion.1 = f32[1152,2048]{1,0:T(8,128)S(1)} fusion(bf16[1152,768]{0,1:T(8,128)(2,1)} %get-tuple-element.16, bf16[1,2048,768]{2,1,0:T(8,128)(2,1)S(1)} %copy-done), kind=kOutput, calls=%fused_computation.17 | convolution fusion | flops 3623878656 | bytes 14352384 | tf_op jit(solution)/shard_map/dot_general | solution.py:8
  305.7 5.7 %add_convert_fusion = bf16[1152,2048]{1,0:T(8,128)(2,1)} fusion(f32[1152,2048]{1,0:T(8,128)S(1)} %fusion.1, bf16[1152,768]{0,1:T(8,128)(2,1)S(1)} %copy-done.9, bf16[1,2048,768]{2,1,0:T(8,128)(2,1)S(1)} %copy-done.5), kind=kOutput, calls=%fused_computation.6 | convolution fusion | flops 3628597248 | bytes 19070976 | tf_op jit(solution)/shard_map/dot_general | solution.py:8
  311.5 8.1 %all_to_all.44 = bf16[128,9,2048]{2,1,0:T(8,128)(2,1)} reshape(bf16[1152,2048]{1,0:T(8,128)(2,1)} %add_convert_fusion) | data formatting | bytes 9437184 | tf_op jit(solution)/shard_map/all_to_all | solution.py:73
  319.6 10.6 %all-to-all-start.3 = ((bf16[128,9,2048]{2,1,0:T(8,128)(2,1)}), bf16[128,9,2048]{2,1,0:T(8,128)(2,1)}, u32[]{:S(2)}, u32[]{:S(2)}) async-start(bf16[128,9,2048]{2,1,0:T(8,128)(2,1)} %all_to_all.44), calls=%async_computation.3 | async-start | bytes 16777216 | tf_op jit(solution)/shard_map/all_to_all | solution.py:73
  330.3 8.2 %fusion.10 = bf16[1,2048,768]{2,1,0:T(8,128)(2,1)} fusion(bf16[1152,2048]{1,0:T(8,128)(2,1)} %all_to_all.43, bf16[1152,768]{0,1:T(8,128)(2,1)S(1)} %copy-done.6), kind=kOutput, calls=%fused_computation.26 | convolution fusion | flops 3625451520 | bytes 9633792 | tf_op jit(solution)/shard_map/dot_general | solution.py:8
  338.5 8.3 %fusion.11 = bf16[1,2048,768]{2,1,0:T(8,128)(2,1)} fusion(bf16[1152,2048]{1,0:T(8,128)(2,1)} %all_to_all.43, bf16[1152,768]{0,1:T(8,128)(2,1)S(1)} %copy-done.10), kind=kOutput, calls=%fused_computation.27 | convolution fusion | flops 3625451520 | bytes 9633792 | tf_op jit(solution)/shard_map/dot_general | solution.py:8
  346.8 5.8 %fusion.12 = bf16[1,768,2048]{2,1,0:T(8,128)(2,1)} fusion(bf16[1152,2048]{1,0:T(8,128)(2,1)S(1)} %bitcast.47, f32[1152]{0:T(1024)S(1)} %reshape.97, f32[1152,768]{0,1:T(8,128)S(1)} %copy-done.8, f32[1152,768]{0,1:T(8,128)S(1)} %copy-done.7), kind=kOutput, calls=%fused_computation.28 | convolution fusion | flops 3631644672 | bytes 14946816 | tf_op jit(solution)/shard_map/dot_general | solution.py:8
  353.0 6.8 %gather_fusion.4 = bf16[1024]{0:T(1024)(128)(2,1)S(1)} fusion(bf16[1152]{0:T(1024)(128)(2,1)S(1)} %all_to_all.48, s32[1024]{0:T(1024)S(1)} %broadcast_clamp_fusion), kind=kCustom, calls=%fused_computation.4 | custom fusion | bytes 8192 | tf_op jit(solution)/shard_map/gather | solution.py:78
  360.6 69.7 %all-to-all-done.3 = bf16[128,9,2048]{2,1,0:T(8,128)(2,1)} async-done(((bf16[128,9,2048]{2,1,0:T(8,128)(2,1)}), bf16[128,9,2048]{2,1,0:T(8,128)(2,1)}, u32[]{:S(2)}, u32[]{:S(2)}) %all-to-all-start.3) | async-done | bytes 4718624 | tf_op jit(solution)/shard_map/all_to_all | solution.py:73
  430.3 8.4 %all_to_all.46 = bf16[1152,2048]{1,0:T(8,128)(2,1)} reshape(bf16[128,9,2048]{2,1,0:T(8,128)(2,1)} %all-to-all-done.3) | data formatting | bytes 9437184 | tf_op jit(solution)/shard_map/all_to_all | solution.py:73
  438.7 11.9 %gather_fusion.3 = bf16[1024,2048]{1,0:T(8,128)(2,1)} fusion(bf16[1152,2048]{1,0:T(8,128)(2,1)} %all_to_all.46, s32[1024]{0:T(1024)S(1)} %broadcast_clamp_fusion), kind=kCustom, calls=%fused_computation.3 | custom fusion | bytes 8392704 | tf_op jit(solution)/shard_map/gather | solution.py:76
  450.6 5.9 %bitcast_reduce_fusion = bf16[128,2048]{1,0:T(8,128)(2,1)} fusion(bf16[1024,2048]{1,0:T(8,128)(2,1)} %gather_fusion.3), kind=kLoop, calls=%fused_computation.7 | loop fusion | flops 1835008 | bytes 4718592 | tf_op jit(solution)/shard_map/reduce_sum | solution.py:77
  (58 shorter events, 8.0 us)
Async XLA Ops:
  0.6 178.8 %copy-start = (bf16[1,2048,768]{2,1,0:T(8,128)(2,1)S(1)}, bf16[1,2048,768]{2,1,0:T(8,128)(2,1)}, u32[]{:S(2)}) copy-start(bf16[1,2048,768]{2,1,0:T(8,128)(2,1)} %param.11) | copy-start | bytes 9437188
  4.0 0.8 copy-start.3
  18.9 32.5 %all-to-all-start = ((bf16[128,9,1]{1,2,0:T(2,128)(2,1)}), bf16[128,9,1]{1,2,0:T(2,128)(2,1)S(1)}, u32[]{:S(2)}, u32[]{:S(2)}) async-start(bf16[128,9,1]{1,2,0:T(2,128)(2,1)} %all_to_all.49), calls=%async_computation | async-start | bytes 131072 | tf_op jit(solution)/shard_map/all_to_all | solution.py:67
  51.4 110.0 %all-to-all-start.2 = ((bf16[128,9,2048]{2,1,0:T(8,128)(2,1)}), bf16[128,9,2048]{2,1,0:T(8,128)(2,1)}, u32[]{:S(2)}, u32[]{:S(2)}) async-start(bf16[128,9,2048]{2,1,0:T(8,128)(2,1)} %all_to_all.41), calls=%async_computation.2 | async-start | bytes 16777216 | tf_op jit(solution)/shard_map/all_to_all | solution.py:65
  161.4 109.2 %all-to-all-start.1 = ((bf16[128,9,2048]{2,1,0:T(8,128)(2,1)}), bf16[128,9,2048]{2,1,0:T(8,128)(2,1)}, u32[]{:S(2)}, u32[]{:S(2)}) async-start(bf16[128,9,2048]{2,1,0:T(8,128)(2,1)} %all_to_all.38), calls=%async_computation.1 | async-start | bytes 16777216 | tf_op jit(solution)/shard_map/all_to_all | solution.py:66
  179.4 8.6 %copy-start.2 = (bf16[1152,2048]{1,0:T(8,128)(2,1)S(1)}, bf16[1152,2048]{1,0:T(8,128)(2,1)}, u32[]{:S(2)}) copy-start(bf16[1152,2048]{1,0:T(8,128)(2,1)} %all_to_all.43) | copy-start | bytes 14155780
  179.4 8.6 %copy-start.4 = (bf16[1,2048,768]{2,1,0:T(8,128)(2,1)S(1)}, bf16[1,2048,768]{2,1,0:T(8,128)(2,1)}, u32[]{:S(2)}) copy-start(bf16[1,2048,768]{2,1,0:T(8,128)(2,1)} %param.12) | copy-start | bytes 9437188
  292.8 26.8 %all-to-all-start.4 = ((bf16[128,9,1]{1,2,0:T(2,128)(2,1)}), bf16[128,9,1]{1,2,0:T(2,128)(2,1)S(1)}, u32[]{:S(2)}, u32[]{:S(2)}) async-start(bf16[128,9,1]{1,2,0:T(2,128)(2,1)} %convert_element_type.67), calls=%async_computation.4 | async-start | bytes 131072 | tf_op jit(solution)/shard_map/all_to_all | solution.py:74
  300.1 5.6 %copy-start.5 = (bf16[1,2048,768]{2,1,0:T(8,128)(2,1)S(1)}, bf16[1,2048,768]{2,1,0:T(8,128)(2,1)}, u32[]{:S(2)}) copy-start(bf16[1,2048,768]{2,1,0:T(8,128)(2,1)} %param.12) | copy-start | bytes 9437188
  300.1 5.6 %copy-start.9 = (bf16[1152,768]{0,1:T(8,128)(2,1)S(1)}, bf16[1152,768]{0,1:T(8,128)(2,1)}, u32[]{:S(2)}) copy-start(bf16[1152,768]{0,1:T(8,128)(2,1)} %get-tuple-element.17) | copy-start | bytes 5308420
  319.6 10.6 %copy-start.6 = (bf16[1152,768]{0,1:T(8,128)(2,1)S(1)}, bf16[1152,768]{0,1:T(8,128)(2,1)}, u32[]{:S(2)}) copy-start(bf16[1152,768]{0,1:T(8,128)(2,1)} %get-tuple-element.16) | copy-start | bytes 5308420
  319.6 110.7 %all-to-all-start.3 = ((bf16[128,9,2048]{2,1,0:T(8,128)(2,1)}), bf16[128,9,2048]{2,1,0:T(8,128)(2,1)}, u32[]{:S(2)}, u32[]{:S(2)}) async-start(bf16[128,9,2048]{2,1,0:T(8,128)(2,1)} %all_to_all.44), calls=%async_computation.3 | async-start | bytes 16777216 | tf_op jit(solution)/shard_map/all_to_all | solution.py:73
  330.2 8.3 %copy-start.10 = (bf16[1152,768]{0,1:T(8,128)(2,1)S(1)}, bf16[1152,768]{0,1:T(8,128)(2,1)}, u32[]{:S(2)}) copy-start(bf16[1152,768]{0,1:T(8,128)(2,1)} %get-tuple-element.17) | copy-start | bytes 5308420
  330.2 16.6 %slice-start = ((s8[4718592]{0:T(1024)(128)(4,1)}), s8[4194304]{0:T(1024)(128)(4,1)S(1)}, s32[]{:S(2)}) async-start(s8[4718592]{0:T(1024)(128)(4,1)} %bitcast.46), calls=%async_computation.5 | async-start | bytes 8388608
  338.5 8.3 %slice-start.1 = ((s8[4718592]{0:T(1024)(128)(4,1)}), s8[524288]{0:T(1024)(128)(4,1)S(1)}, s32[]{:S(2)}) async-start(s8[4718592]{0:T(1024)(128)(4,1)} %bitcast.46), calls=%async_computation.6 | async-start | bytes 1048576
  338.5 8.3 %copy-start.7 = (f32[1152,768]{0,1:T(8,128)S(1)}, f32[1152,768]{0,1:T(8,128)}, u32[]{:S(2)}) copy-start(f32[1152,768]{0,1:T(8,128)} %fusion.3) | copy-start | bytes 10616836
  338.5 8.3 %copy-start.8 = (f32[1152,768]{0,1:T(8,128)S(1)}, f32[1152,768]{0,1:T(8,128)}, u32[]{:S(2)}) copy-start(f32[1152,768]{0,1:T(8,128)} %fusion.6) | copy-start | bytes 10616836
  438.7 17.8 %copy-start.1 = (bf16[1,2048,768]{2,1,0:T(8,128)(2,1)S(1)}, bf16[1,2048,768]{2,1,0:T(8,128)(2,1)}, u32[]{:S(2)}) copy-start(bf16[1,2048,768]{2,1,0:T(8,128)(2,1)} %param.11) | copy-start | bytes 9437188
where the time goes:
time: 465 us; the launch traced here: 457 us
  waiting for transfers between devices  224 us (48%)
  local copies, waits for them, and re-layouts  114 us (25%)
  matrix products  61.1 us (13%)
  starting transfers between devices  48 us (10%)
  other arithmetic  8.8 us (2%)
    all_to_all x1, waiting for transfers between devices, body(): lax.all_to_all(send_acts, ('grp', 'loc'), split_axis=0, concat_axis=0, ti...  78 us
    all_to_all x1, waiting for transfers between devices, body(): lax.all_to_all(send_grad, ('grp', 'loc'), split_axis=0, concat_axis=0, ti...  76.4 us
    all_to_all x1, waiting for transfers between devices, body(): lax.all_to_all(input_grad, ('grp', 'loc'), split_axis=0, concat_axis=0, t...  69.7 us
    dot_general x6, matrix products, contract(): lax.dot_general(left, right, (((left_dim,), (right_dim,)), ((), ())), pre...  46.3 us
    all_to_all x2, local copies, waits for them, and re-layouts, body(): lax.all_to_all(send_grad, ('grp', 'loc'), split_axis=0, concat_axis=0, ti...  16.7 us
    all_to_all x2, local copies, waits for them, and re-layouts, body(): lax.all_to_all(send_acts, ('grp', 'loc'), split_axis=0, concat_axis=0, ti...  16.6 us
    all_to_all x2, local copies, waits for them, and re-layouts, body(): lax.all_to_all(input_grad, ('grp', 'loc'), split_axis=0, concat_axis=0, t...  16.5 us
    gather x1, local copies, waits for them, and re-layouts, body(): back_rows[slot_of].reshape(tokens, top_count, width).astype(jnp.float32)  11.9 us
  transfers between devices with their start and end apart: 5, of which 3 were waited for; matrix products, arithmetic and copies ran while one was open for 18% of the time, Pallas kernels for 0%

commit v1 on v0

v1 whole, which is shorter than its diff:
```python
import functools

import jax
import jax.numpy as jnp
from jax import lax
from jax.experimental import pallas as pl
from jax.experimental.pallas import tpu as pltpu
from jax.sharding import PartitionSpec as P

AXES = ("grp", "loc")
BF = jnp.bfloat16
F32 = jnp.float32
E = 128
T = 128
R8 = 1024
ROWS = 1152
D = 2048
FF = 768
LANE = 128
SUB = 8
FOLD = D // SUB
WIDE = D + FOLD
WIDE_G = WIDE + LANE
TN = 512
PIECES = TN // FOLD


def dot(a, b, ca=1, cb=0):
    return lax.dot_general(a, b, (((ca,), (cb,)), ((), ())), preferred_element_type=F32)


def nine_rows(i):
    return pl.ds(i, E, stride=SUB)


def fold_in(fold, i, value):
    for h in range(FOLD // LANE):
        fold[h, nine_rows(i), :] = value[:, h * LANE : (h + 1) * LANE]


def fold_out(fold, i):
    return jnp.concatenate(
        [fold[h, nine_rows(i), :] for h in range(FOLD // LANE)], axis=1
    )


def params(steps=1, limit=None):
    return pltpu.CompilerParams(
        dimension_semantics=("arbitrary",) * steps, vmem_limit_bytes=limit
    )


def cost(flops, bytes_accessed):
    return pl.CostEstimate(
        flops=int(flops), bytes_accessed=int(bytes_accessed), transcendentals=0
    )


def pack_acts_kernel(ids_ref, gates_ref, x_ref, out_ref, sel_ref, sel9_ref, fold, gate_blk):
    j = pl.program_id(0)

    @pl.when(j == 0)
    def _():
        expert = lax.broadcasted_iota(jnp.int32, (E, T), 0)
        member = jnp.zeros((E, T), F32)
        gate = jnp.zeros((E, T), F32)
        for k in range(8):
            hit = ids_ref[k : k + 1, :] == expert
            member = jnp.where(hit, 1.0, member)
            gate = jnp.where(hit, gates_ref[k : k + 1, :].astype(F32), gate)
        earlier = (
            lax.broadcasted_iota(jnp.int32, (T, T), 0)
            < lax.broadcasted_iota(jnp.int32, (T, T), 1)
        ).astype(F32)
        rank = dot(member.astype(BF), earlier.astype(BF))
        rank = jnp.where(member > 0.0, rank, -1.0)
        slot = lax.broadcasted_iota(jnp.int32, (E, SUB, T), 1).astype(F32)
        sel = jnp.where(rank[:, None, :] == slot, 1.0, 0.0)
        sel9 = jnp.where(rank == float(SUB), 1.0, 0.0)
        sel_gate = (sel * gate[:, None, :]).reshape(R8, T)
        sel_ref[...] = sel.reshape(R8, T).astype(BF)
        sel9_ref[...] = sel9.astype(BF)
        ones = jnp.ones((T, LANE), BF)
        own = dot(sel_gate.astype(BF), ones)
        ninth = dot((sel9 * gate).astype(BF), ones)
        ninth = jnp.broadcast_to(ninth[:, None, :], (E, SUB, LANE)).reshape(R8, LANE)
        lane = lax.broadcasted_iota(jnp.int32, (R8, LANE), 1)
        gate_blk[...] = jnp.where(lane == 1, ninth, own).astype(BF)

    @pl.when(j < D // TN)
    def _():
        x = x_ref[...]
        out_ref[...] = dot(sel_ref[...], x).astype(BF)
        nine = dot(sel9_ref[...], x)
        for p in range(PIECES):
            fold_in(fold, j * PIECES + p, nine[:, p * FOLD : (p + 1) * FOLD])

    @pl.when(j == D // TN)
    def _():
        for h in range(FOLD // LANE):
            out_ref[:, h * LANE : (h + 1) * LANE] = fold[h].astype(BF)
        out_ref[:, FOLD : FOLD + LANE] = gate_blk[...]


def pack_acts(ids_t, gates_t, acts):
    last = D // TN - 1
    return pl.pallas_call(
        pack_acts_kernel,
        grid=(D // TN + 1,),
        in_specs=[
            pl.BlockSpec((8, T), lambda j: (0, 0)),
            pl.BlockSpec((8, T), lambda j: (0, 0)),
            pl.BlockSpec((T, TN), lambda j: (0, jnp.minimum(j, last))),
        ],
        out_specs=[
            pl.BlockSpec((R8, TN), lambda j: (0, j)),
            pl.BlockSpec((R8, T), lambda j: (0, 0)),
            pl.BlockSpec((E, T), lambda j: (0, 0)),
        ],
        out_shape=[
            jax.ShapeDtypeStruct((R8, WIDE_G), BF),
            jax.ShapeDtypeStruct((R8, T), BF),
            jax.ShapeDtypeStruct((E, T), BF),
        ],
        scratch_shapes=[
            pltpu.VMEM((FOLD // LANE, R8, LANE), F32),
            pltpu.VMEM((R8, LANE), BF),
        ],
        compiler_params=params(),
        cost_estimate=cost(2 * ROWS * T * D, 2 * (R8 * WIDE_G + T * D)),
        name="pack_acts",
    )(ids_t, gates_t, acts)


def pack_grad_kernel(sel_ref, sel9_ref, x_ref, out_ref, fold):
    j = pl.program_id(0)

    @pl.when(j < D // TN)
    def _():
        x = x_ref[...]
        out_ref[...] = dot(sel_ref[...], x).astype(BF)
        nine = dot(sel9_ref[...], x)
        for p in range(PIECES):
            fold_in(fold, j * PIECES + p, nine[:, p * FOLD : (p + 1) * FOLD])

    @pl.when(j == D // TN)
    def _():
        for h in range(FOLD // LANE):
            out_ref[:, h * LANE : (h + 1) * LANE] = fold[h].astype(BF)


def pack_grad(sel, sel9, grad):
    last = D // TN - 1
    return pl.pallas_call(
        pack_grad_kernel,
        grid=(D // TN + 1,),
        in_specs=[
            pl.BlockSpec((R8, T), lambda j: (0, 0)),
            pl.BlockSpec((E, T), lambda j: (0, 0)),
            pl.BlockSpec((T, TN), lambda j: (0, jnp.minimum(j, last))),
        ],
        out_specs=pl.BlockSpec((R8, TN), lambda j: (0, j)),
        out_shape=jax.ShapeDtypeStruct((R8, WIDE), BF),
        scratch_shapes=[pltpu.VMEM((FOLD // LANE, R8, LANE), F32)],
        compiler_params=params(),
        cost_estimate=cost(2 * ROWS * T * D, 2 * (R8 * WIDE + T * D)),
        name="pack_grad",
    )(sel, sel9, grad)


TF = 256
MB = 384


def unfold(fold, y_ref, rows_ref):
    rows_ref[0:R8, :] = y_ref[:, 0:D]
    for h in range(FOLD // LANE):
        fold[h] = y_ref[:, D + h * LANE : D + (h + 1) * LANE].astype(F32)
    for i in range(SUB):
        rows_ref[R8:ROWS, i * FOLD : (i + 1) * FOLD] = fold_out(fold, i).astype(BF)


def acts_kernel(y_ref, wg_ref, wu_ref, rows_ref, a_ref, b_ref, hid_ref, hw_ref, fold, gcol):
    i = pl.program_id(0)

    @pl.when(i == 0)
    def _():
        unfold(fold, y_ref, rows_ref)
        fold[0] = y_ref[:, WIDE:WIDE_G].astype(F32)
        gcol[0:R8, :] = jnp.broadcast_to(fold[0, :, 0:1], (R8, LANE))
        ninth = fold[0, nine_rows(0), :]
        gcol[R8:ROWS, :] = jnp.broadcast_to(ninth[:, 1:2], (E, LANE))

    for m in range(ROWS // MB):
        rows = pl.ds(m * MB, MB)
        x = rows_ref[rows, :]
        pre = dot(x, wg_ref[...])
        up = dot(x, wu_ref[...])
        gate = jnp.concatenate([gcol[rows, :]] * (TF // LANE), axis=1)
        s = jax.nn.sigmoid(pre)
        act = pre * s
        hid = act * up
        hid_ref[rows, :] = hid
        hw_ref[rows, :] = (gate * hid).astype(BF)
        a_ref[rows, :] = gate * (up * s * (1.0 + pre * (1.0 - s)))
        b_ref[rows, :] = gate * act


def acts_side(y, wg, wu):
    tile = lambda i: (0, i)
    return pl.pallas_call(
        acts_kernel,
        grid=(FF // TF,),
        in_specs=[
            pl.BlockSpec((R8, WIDE_G), lambda i: (0, 0), pipeline_mode=pl.Buffered(1)),
            pl.BlockSpec((D, TF), tile),
            pl.BlockSpec((D, TF), tile),
        ],
        out_specs=[
            pl.BlockSpec((ROWS, D), lambda i: (0, 0), pipeline_mode=pl.Buffered(1)),
            pl.BlockSpec((ROWS, TF), tile),
            pl.BlockSpec((ROWS, TF), tile),
            pl.BlockSpec((ROWS, TF), tile),
            pl.BlockSpec((ROWS, TF), tile),
        ],
        out_shape=[
            jax.ShapeDtypeStruct((ROWS, D), BF),
            jax.ShapeDtypeStruct((ROWS, FF), F32),
            jax.ShapeDtypeStruct((ROWS, FF), F32),
            jax.ShapeDtypeStruct((ROWS, FF), F32),
            jax.ShapeDtypeStruct((ROWS, FF), BF),
        ],
        scratch_shapes=[
            pltpu.VMEM((FOLD // LANE, R8, LANE), F32),
            pltpu.VMEM((ROWS, LANE), F32),
        ],
        compiler_params=params(),
        cost_estimate=cost(4 * ROWS * D * FF, 30e6),
        name="acts_side",
    )(y, wg, wu)


N1 = FF // TF
N2 = D // TN


def grads_kernel(
    y_ref, wd_ref, a_ref, b_ref, hid_ref, wg_ref, wu_ref,
    out_ref, rows_ref, dpre_ref, dup_ref, fold, gsum,
):
    i = pl.program_id(0)

    @pl.when(i == 0)
    def _():
        unfold(fold, y_ref, rows_ref)
        gsum[...] = jnp.zeros_like(gsum)

    @pl.when(i < N1)
    def _():
        cols = pl.ds(pl.multiple_of(jnp.minimum(i, N1 - 1) * TF, TF), TF)
        for m in range(ROWS // MB):
            rows = pl.ds(m * MB, MB)
            dh = dot(rows_ref[rows, :], wd_ref[...], 1, 1)
            gg = hid_ref[rows, :] * dh
            gsum[rows, :] += gg[:, 0:LANE] + gg[:, LANE:TF]
            dpre_ref[rows, cols] = (dh * a_ref[rows, :]).astype(BF)
            dup_ref[rows, cols] = (dh * b_ref[rows, :]).astype(BF)

    @pl.when((i >= N1) & (i < N1 + N2))
    def _():
        for m in range(ROWS // MB):
            rows = pl.ds(m * MB, MB)
            dx = dot(dpre_ref[rows, :], wg_ref[...], 1, 1)
            dx = dx + dot(dup_ref[rows, :], wu_ref[...], 1, 1)
            keep = min(MB, R8 - m * MB)
            out_ref[m * MB : m * MB + keep, :] = dx[0:keep].astype(BF)
            if keep < MB:
                for p in range(PIECES):
                    fold_in(
                        fold,
                        (i - N1) * PIECES + p,
                        dx[keep:MB, p * FOLD : (p + 1) * FOLD],
                    )

    @pl.when(i == N1 + N2)
    def _():
        for h in range(FOLD // LANE):
            out_ref[:, h * LANE : (h + 1) * LANE] = fold[h].astype(BF)
        total = jnp.sum(gsum[...], axis=1, keepdims=True)
        ninth = jnp.broadcast_to(total[R8:ROWS], (E, LANE))
        for s in range(SUB):
            fold[0, nine_rows(s), :] = ninth
        lane = lax.broadcasted_iota(jnp.int32, (R8, LANE), 1)
        own = jnp.broadcast_to(total[0:R8], (R8, LANE))
        out_ref[:, FOLD : FOLD + LANE] = jnp.where(lane == 1, fold[0], own).astype(BF)


def grads_side(y, wd, a, b, hid, wg, wu):
    first = lambda i: (0, jnp.minimum(i, N1 - 1))
    second = lambda i: (jnp.clip(i - N1, 0, N2 - 1), 0)
    whole = lambda i: (0, 0)
    one = pl.Buffered(1)
    return pl.pallas_call(
        grads_kernel,
        grid=(N1 + N2 + 1,),
        in_specs=[
            pl.BlockSpec((R8, WIDE), whole, pipeline_mode=one),
            pl.BlockSpec((TF, D), lambda i: (jnp.minimum(i, N1 - 1), 0)),
            pl.BlockSpec((ROWS, TF), first),
            pl.BlockSpec((ROWS, TF), first),
            pl.BlockSpec((ROWS, TF), first),
            pl.BlockSpec((TN, FF), second),
            pl.BlockSpec((TN, FF), second),
        ],
        out_specs=[
            pl.BlockSpec((R8, TN), lambda i: (0, jnp.maximum(i - N1, 0))),
            pl.BlockSpec((ROWS, D), whole, pipeline_mode=one),
            pl.BlockSpec((ROWS, FF), whole, pipeline_mode=one),
            pl.BlockSpec((ROWS, FF), whole, pipeline_mode=one),
        ],
        out_shape=[
            jax.ShapeDtypeStruct((R8, WIDE_G), BF),
            jax.ShapeDtypeStruct((ROWS, D), BF),
            jax.ShapeDtypeStruct((ROWS, FF), BF),
            jax.ShapeDtypeStruct((ROWS, FF), BF),
        ],
        scratch_shapes=[
            pltpu.VMEM((FOLD // LANE, R8, LANE), F32),
            pltpu.VMEM((ROWS, LANE), F32),
        ],
        compiler_params=params(),
        cost_estimate=cost(6 * ROWS * D * FF, 36e6),
        name="grads_side",
    )(y, wd, a, b, hid, wg, wu)


def combine_kernel(ids_ref, sel_ref, sel9_ref, y_ref, y9_ref, yg_ref, out_ref, gg_ref, fold):
    j = pl.program_id(0)

    @pl.when(j == 0)
    def _():
        fold[0] = yg_ref[...].astype(F32)
        own = jnp.broadcast_to(fold[0, :, 0:1], (R8, T))
        ninth = jnp.broadcast_to(fold[0, nine_rows(0), :][:, 1:2], (E, T))
        sel = sel_ref[...].astype(F32)
        picked = jnp.where(sel > 0.0, own, 0.0).reshape(E, SUB, T)
        table = jnp.sum(picked, axis=1)
        table = table + jnp.where(sel9_ref[...].astype(F32) > 0.0, ninth, 0.0)
        expert = lax.broadcasted_iota(jnp.int32, (E, T), 0)
        for k in range(8):
            hit = ids_ref[k : k + 1, :] == expert
            gg_ref[k : k + 1, :] = jnp.sum(
                jnp.where(hit, table, 0.0), axis=0, keepdims=True
            )
        for h in range(FOLD // LANE):
            fold[h] = y9_ref[:, h * LANE : (h + 1) * LANE].astype(F32)

    acc = dot(sel_ref[...], y_ref[...], 0, 0)
    nine = jnp.concatenate(
        [fold_out(fold, j * PIECES + p) for p in range(PIECES)], axis=1
    ).astype(BF)
    out_ref[...] = (acc + dot(sel9_ref[...], nine, 0, 0)).astype(BF)


def combine(ids_t, sel, sel9, y):
    whole = lambda j: (0, 0)
    return pl.pallas_call(
        combine_kernel,
        grid=(D // TN,),
        in_specs=[
            pl.BlockSpec((8, T), whole),
            pl.BlockSpec((R8, T), whole),
            pl.BlockSpec((E, T), whole),
            pl.BlockSpec((R8, TN), lambda j: (0, j)),
            pl.BlockSpec((R8, FOLD), lambda j: (0, D // FOLD)),
            pl.BlockSpec((R8, LANE), lambda j: (0, WIDE // LANE)),
        ],
        out_specs=[
            pl.BlockSpec((T, TN), lambda j: (0, j)),
            pl.BlockSpec((8, T), whole),
        ],
        out_shape=[
            jax.ShapeDtypeStruct((T, D), BF),
            jax.ShapeDtypeStruct((8, T), F32),
        ],
        scratch_shapes=[pltpu.VMEM((FOLD // LANE, R8, LANE), F32)],
        compiler_params=params(),
        cost_estimate=cost(2 * ROWS * T * D, 2 * (R8 * WIDE_G + T * D)),
        name="combine",
    )(ids_t, sel, sel9, y, y, y)


def exchange(x):
    width = x.shape[1]
    y = lax.all_to_all(
        x.reshape(E, SUB, width), AXES, split_axis=0, concat_axis=0, tiled=True
    )
    return y.reshape(R8, width)


def body(acts, out_grad, expert_ids, gate_vals, w_gate, w_up, w_down):
    ids_t = expert_ids.T
    gates_t = gate_vals.T
    wg, wu, wd = w_gate[0], w_up[0], w_down[0]
    send_acts, sel, sel9 = pack_acts(ids_t, gates_t, acts)
    got_acts = exchange(send_acts)
    send_grad = pack_grad(sel, sel9, out_grad)
    got_grad = exchange(send_grad)
    rows_in, coef_pre, coef_up, hidden, scaled = acts_side(got_acts, wg, wu)
    back, rows_grad, dpre, dup = grads_side(
        got_grad, wd, coef_pre, coef_up, hidden, wg, wu
    )
    got_back = exchange(back)
    wg_grad = dot(rows_in, dpre, 0, 0).astype(BF)
    wu_grad = dot(rows_in, dup, 0, 0).astype(BF)
    wd_grad = dot(scaled, rows_grad, 0, 0).astype(BF)
    grad_acts, gate_grad_t = combine(ids_t, sel, sel9, got_back)
    return (
        grad_acts,
        gate_grad_t.astype(BF).T,
        wg_grad[None],
        wu_grad[None],
        wd_grad[None],
    )


def solution(mesh):
    rows = P(AXES, None)
    mats = P(AXES, None, None)
    return jax.shard_map(
        body,
        mesh=mesh,
        in_specs=(rows, rows, rows, rows, mats, mats, mats),
        out_specs=(rows, rows, mats, mats, mats),
        check_vma=False,
    )
```

time: 465 us -> 241 us (0.52)
  local copies, waits for them, and re-layouts: 114 us -> 0.04 us
  waiting for transfers between devices: 224 us -> 133 us
  Pallas kernels: 0 us -> 54.4 us
  matrix products: 61.1 us -> 19.6 us
  starting transfers between devices: 48 us -> 27.5 us
  other arithmetic: 8.8 us -> 1.25 us
    all_to_all x5 -> x3, waiting for transfers between devices: 224 us -> 133 us  [exchange(): lax.all_to_all(x.reshape(E, SUB, width), AXES, split_axis=0, concat_axis=...]
    pallas_call x0 -> x5, Pallas kernels: none -> 54.4 us  [the longest x1 23.4 us: grads_side(): pl.pallas_call(grads_kernel, grid=(N1 + N2 + 1,), in_specs=[pl.BlockSpec(...]
    all_to_all x8 -> x0, local copies, waits for them, and re-layouts: 50.9 us -> none  [the longest x2 16.7 us: body(): lax.all_to_all(send_grad, ('grp', 'loc'), split_axis=0, concat_axis=0, ti...]
    gather x5 -> x0, local copies, waits for them, and re-layouts: 49.6 us -> none  [the longest x1 11.9 us: body(): back_rows[slot_of].reshape(tokens, top_count, width).astype(jnp.float32)]
    dot_general x8 -> x3, matrix products: 61.1 us -> 19.6 us  [dot(): lax.dot_general(a, b, (((ca,), (cb,)), ((), ())), preferred_element_type=...]
    all_to_all x5 -> x3, starting transfers between devices: 48 us -> 27.5 us  [exchange(): lax.all_to_all(x.reshape(E, SUB, width), AXES, split_axis=0, concat_axis=...]
    reduce_sum x2 -> x0, other arithmetic: 6.24 us -> none  [the longest x1 5.88 us: body(): grad_acts = jnp.sum(picked, axis=1).astype(jnp.bfloat16)]
  transfers between devices with their start and end apart: 5 -> 3, of which waited for: 3 -> 3; matrix products, arithmetic and copies ran while one was open for 18% -> 8% of each run, Pallas kernels for 0% -> 8%
where the time goes in v1:
time: 241 us; the launch traced here: 237 us
  waiting for transfers between devices  133 us (55%)
  Pallas kernels  54.4 us (23%)
  starting transfers between devices  27.5 us (11%)
  matrix products  19.6 us (8%)
    all_to_all x3, waiting for transfers between devices, exchange(): lax.all_to_all(x.reshape(E, SUB, width), AXES, split_axis=0, concat_axis=...  133 us
    all_to_all x3, starting transfers between devices, exchange(): lax.all_to_all(x.reshape(E, SUB, width), AXES, split_axis=0, concat_axis=...  27.5 us
    pallas_call x1, Pallas kernels, grads_side(): pl.pallas_call(grads_kernel, grid=(N1 + N2 + 1,), in_specs=[pl.BlockSpec(...  23.4 us
    dot_general x3, matrix products, dot(): lax.dot_general(a, b, (((ca,), (cb,)), ((), ())), preferred_element_type=...  19.6 us
    pallas_call x1, Pallas kernels, acts_side(): pl.pallas_call(acts_kernel, grid=(FF // TF,), in_specs=[pl.BlockSpec((R8,...  14.6 us
    pallas_call x1, Pallas kernels, pack_acts(): pl.pallas_call(pack_acts_kernel, grid=(D // TN + 1,), in_specs=[pl.BlockS...  5.81 us
    pallas_call x1, Pallas kernels, combine(): pl.pallas_call(combine_kernel, grid=(D // TN,), in_specs=[pl.BlockSpec((8...  5.32 us
    pallas_call x1, Pallas kernels, pack_grad(): pl.pallas_call(pack_grad_kernel, grid=(D // TN + 1,), in_specs=[pl.BlockS...  5.25 us
  transfers between devices with their start and end apart: 3, of which 3 were waited for; matrix products, arithmetic and copies ran while one was open for 8% of the time, Pallas kernels for 8%

profile of v1, /device:TPU:13, one launch (start us, length us, event | category | flops | bytes accessed | tf_op | source)
XLA Modules:
  0.0 237.0 jit_solution(2400149582206168321)
XLA Ops:
  0.6 5.8 %pack_acts.1 = (bf16[1024,2432]{1,0:T(8,128)(2,1)}, bf16[1024,128]{1,0:T(8,128)(2,1)}, bf16[128,128]{1,0:T(8,128)(2,1)}) custom-call(s32[8,128]{1,0:T(8,128)} %bitcast.28, bf16[8,128]{1,0:T(8,128)(2,1)} %bitcast.35, bf16[128,2048]{1,0:T(8,128)(2,1)} %x_ref.2), custom_call_target="tpu_custom_call" | custom-call | flops 603979776 | bytes 5505024 | tf_op jit(solution)/shard_map/pack_acts/pallas_call | solution.py:107
  6.4 11.1 %all-to-all-start.1 = ((bf16[128,8,2432]{2,1,0:T(8,128)(2,1)}), bf16[128,8,2432]{2,1,0:T(8,128)(2,1)}, u32[]{:S(2)}, u32[]{:S(2)}) async-start(bf16[128,8,2432]{2,1,0:T(8,128)(2,1)} %bitcast.27), calls=%async_computation.1 | async-start | bytes 9961472 | tf_op jit(solution)/shard_map/all_to_all | solution.py:395
  17.5 5.3 %pack_grad.1 = bf16[1024,2304]{1,0:T(8,128)(2,1)} custom-call(bf16[1024,128]{1,0:T(8,128)(2,1)} %get-tuple-element.19.sel_ref, bf16[128,128]{1,0:T(8,128)(2,1)} %get-tuple-element.20.sel9_ref, bf16[128,2048]{1,0:T(8,128)(2,1)} %x_ref.3), custom_call_target="tpu_custom_call" | custom-call | flops 603979776 | bytes 5242880 | tf_op jit(solution)/shard_map/pack_grad/pallas_call | solution.py:154
  22.8 53.4 %all-to-all-done.1 = bf16[128,8,2432]{2,1,0:T(8,128)(2,1)} async-done(((bf16[128,8,2432]{2,1,0:T(8,128)(2,1)}), bf16[128,8,2432]{2,1,0:T(8,128)(2,1)}, u32[]{:S(2)}, u32[]{:S(2)}) %all-to-all-start.1) | async-done | bytes 4980768 | tf_op jit(solution)/shard_map/all_to_all | solution.py:395
  76.1 8.1 %all-to-all-start = ((bf16[128,8,2304]{2,1,0:T(8,128)(2,1)}), bf16[128,8,2304]{2,1,0:T(8,128)(2,1)}, u32[]{:S(2)}, u32[]{:S(2)}) async-start(bf16[128,8,2304]{2,1,0:T(8,128)(2,1)} %bitcast.25), calls=%async_computation | async-start | bytes 9437184 | tf_op jit(solution)/shard_map/all_to_all | solution.py:395
  84.3 14.6 %acts_side.1 = (bf16[1152,2048]{1,0:T(8,128)(2,1)}, f32[1152,768]{1,0:T(8,128)}, f32[1152,768]{1,0:T(8,128)}, f32[1152,768]{1,0:T(8,128)}, bf16[1152,768]{1,0:T(8,128)(2,1)}) custom-call(bf16[1024,2432]{1,0:T(8,128)(2,1)} %bitcast.6.y_ref, bf16[2048,768]{1,0:T(8,128)(2,1)} %bitcast.31, bf16[2048,768]{1,0:T(8,128)(2,1)} %bitcast.33), custom_call_target="tpu_custom_call" | custom-call | flops 7247757312 | bytes 30000000 | tf_op jit(solution)/shard_map/acts_side/pallas_call | solution.py:211
  98.9 41.1 %all-to-all-done = bf16[128,8,2304]{2,1,0:T(8,128)(2,1)} async-done(((bf16[128,8,2304]{2,1,0:T(8,128)(2,1)}), bf16[128,8,2304]{2,1,0:T(8,128)(2,1)}, u32[]{:S(2)}, u32[]{:S(2)}) %all-to-all-start) | async-done | bytes 4718624 | tf_op jit(solution)/shard_map/all_to_all | solution.py:395
  140.0 23.4 %grads_side.1 = (bf16[1024,2432]{1,0:T(8,128)(2,1)}, bf16[1152,2048]{1,0:T(8,128)(2,1)}, bf16[1152,768]{1,0:T(8,128)(2,1)}, bf16[1152,768]{1,0:T(8,128)(2,1)}) custom-call(bf16[1024,2304]{1,0:T(8,128)(2,1)} %bitcast.3.y_ref, bf16[768,2048]{1,0:T(8,128)(2,1)} %bitcast.30, f32[1152,768]{1,0:T(8,128)} %get-tuple-element.22.a_ref, ...), custom_call_target="tpu_custom_call" | custom-call | flops 10871635968 | bytes 36000000 | tf_op jit(solution)/shard_map/grads_side/pallas_call | solution.py:303
  163.4 0.0 copy-start.2
  163.4 0.0 slice-start.2
  163.5 8.3 %all-to-all-start.2 = ((bf16[128,8,2432]{2,1,0:T(8,128)(2,1)}), bf16[128,8,2432]{2,1,0:T(8,128)(2,1)}, u32[]{:S(2)}, u32[]{:S(2)}) async-start(bf16[128,8,2432]{2,1,0:T(8,128)(2,1)} %bitcast.26), calls=%async_computation.2 | async-start | bytes 9961472 | tf_op jit(solution)/shard_map/all_to_all | solution.py:395
  171.8 0.0 copy-done.2
  171.8 0.0 slice-start.3
  171.8 0.0 copy-start.1
  171.8 0.0 slice-start
  171.9 8.3 %fusion = bf16[1,2048,768]{2,1,0:T(8,128)(2,1)} fusion(bf16[1152,2048]{1,0:T(8,128)(2,1)} %get-tuple-element.28, bf16[1152,768]{1,0:T(8,128)(2,1)S(1)} %copy-done.2), kind=kOutput, calls=%fused_computation.3 | convolution fusion | flops 3625451520 | bytes 9633792 | tf_op jit(solution)/shard_map/dot_general | solution.py:29
  180.1 0.0 slice-done.2
  180.1 0.0 slice-done.3
  180.1 0.0 copy-done.1
  180.1 0.0 slice-start.1
  180.1 0.0 copy-start
  180.2 5.7 %fusion.1 = bf16[1,2048,768]{2,1,0:T(8,128)(2,1)} fusion(bf16[1152,2048]{1,0:T(8,128)(2,1)S(1)} %bitcast.39, bf16[1152,768]{1,0:T(8,128)(2,1)S(1)} %copy-done.1), kind=kOutput, calls=%fused_computation.4 | convolution fusion | flops 3625451520 | bytes 9633792 | tf_op jit(solution)/shard_map/dot_general | solution.py:29
  185.9 0.0 slice-done
  185.9 0.0 slice-done.1
  185.9 0.0 copy-done
  185.9 5.6 %fusion.2 = bf16[1,768,2048]{2,1,0:T(8,128)(2,1)} fusion(bf16[1152,768]{1,0:T(8,128)(2,1)S(1)} %copy-done, bf16[1152,2048]{1,0:T(8,128)(2,1)S(1)} %bitcast.37), kind=kOutput, calls=%fused_computation.5 | convolution fusion | flops 3625451520 | bytes 9633792 | tf_op jit(solution)/shard_map/dot_general | solution.py:29
  191.6 38.9 %all-to-all-done.2 = bf16[128,8,2432]{2,1,0:T(8,128)(2,1)} async-done(((bf16[128,8,2432]{2,1,0:T(8,128)(2,1)}), bf16[128,8,2432]{2,1,0:T(8,128)(2,1)}, u32[]{:S(2)}, u32[]{:S(2)}) %all-to-all-start.2) | async-done | bytes 4980768 | tf_op jit(solution)/shard_map/all_to_all | solution.py:395
  230.5 5.3 %combine.1 = (bf16[128,2048]{1,0:T(8,128)(2,1)}, f32[8,128]{1,0:T(8,128)}) custom-call(s32[8,128]{1,0:T(8,128)} %bitcast.29, bf16[1024,128]{1,0:T(8,128)(2,1)} %get-tuple-element.19.sel_ref, bf16[128,128]{1,0:T(8,128)(2,1)} %get-tuple-element.20.sel9_ref, bf16[1024,2432]{1,0:T(8,128)(2,1)} %bitcast.10.y_ref.y9_ref.yg_ref, ...), custom_call_target="tpu_custom_call" | custom-call | flops 603979776 | bytes 5505024 | tf_op jit(solution)/shard_map/combine/pallas_call | solution.py:367
  235.8 1.3 convert_bitcast_fusion
  (2 shorter events, 0.0 us)
Async XLA Ops:
  6.4 69.7 %all-to-all-start.1 = ((bf16[128,8,2432]{2,1,0:T(8,128)(2,1)}), bf16[128,8,2432]{2,1,0:T(8,128)(2,1)}, u32[]{:S(2)}, u32[]{:S(2)}) async-start(bf16[128,8,2432]{2,1,0:T(8,128)(2,1)} %bitcast.27), calls=%async_computation.1 | async-start | bytes 9961472 | tf_op jit(solution)/shard_map/all_to_all | solution.py:395
  76.1 63.9 %all-to-all-start = ((bf16[128,8,2304]{2,1,0:T(8,128)(2,1)}), bf16[128,8,2304]{2,1,0:T(8,128)(2,1)}, u32[]{:S(2)}, u32[]{:S(2)}) async-start(bf16[128,8,2304]{2,1,0:T(8,128)(2,1)} %bitcast.25), calls=%async_computation | async-start | bytes 9437184 | tf_op jit(solution)/shard_map/all_to_all | solution.py:395
  163.4 8.4 %copy-start.2 = (bf16[1152,768]{1,0:T(8,128)(2,1)S(1)}, bf16[1152,768]{1,0:T(8,128)(2,1)}, u32[]{:S(2)}) copy-start(bf16[1152,768]{1,0:T(8,128)(2,1)} %get-tuple-element.29) | copy-start | bytes 5308420
  163.4 16.7 %slice-start.2 = ((s8[4718592]{0:T(1024)(128)(4,1)}), s8[524288]{0:T(1024)(128)(4,1)S(1)}, s32[]{:S(2)}) async-start(s8[4718592]{0:T(1024)(128)(4,1)} %bitcast.38), calls=%async_computation.5 | async-start | bytes 1048576
  163.5 67.0 %all-to-all-start.2 = ((bf16[128,8,2432]{2,1,0:T(8,128)(2,1)}), bf16[128,8,2432]{2,1,0:T(8,128)(2,1)}, u32[]{:S(2)}, u32[]{:S(2)}) async-start(bf16[128,8,2432]{2,1,0:T(8,128)(2,1)} %bitcast.26), calls=%async_computation.2 | async-start | bytes 9961472 | tf_op jit(solution)/shard_map/all_to_all | solution.py:395
  171.8 8.3 %slice-start.3 = ((s8[4718592]{0:T(1024)(128)(4,1)}), s8[4194304]{0:T(1024)(128)(4,1)S(1)}, s32[]{:S(2)}) async-start(s8[4718592]{0:T(1024)(128)(4,1)} %bitcast.38), calls=%async_computation.6 | async-start | bytes 8388608
  171.8 8.3 %copy-start.1 = (bf16[1152,768]{1,0:T(8,128)(2,1)S(1)}, bf16[1152,768]{1,0:T(8,128)(2,1)}, u32[]{:S(2)}) copy-start(bf16[1152,768]{1,0:T(8,128)(2,1)} %get-tuple-element.30) | copy-start | bytes 5308420
  171.8 14.0 %slice-start = ((s8[4718592]{0:T(1024)(128)(4,1)}), s8[4194304]{0:T(1024)(128)(4,1)S(1)}, s32[]{:S(2)}) async-start(s8[4718592]{0:T(1024)(128)(4,1)} %bitcast.36), calls=%async_computation.3 | async-start | bytes 8388608
  180.1 5.8 %slice-start.1 = ((s8[4718592]{0:T(1024)(128)(4,1)}), s8[524288]{0:T(1024)(128)(4,1)S(1)}, s32[]{:S(2)}) async-start(s8[4718592]{0:T(1024)(128)(4,1)} %bitcast.36), calls=%async_computation.4 | async-start | bytes 1048576
  180.1 5.7 %copy-start = (bf16[1152,768]{1,0:T(8,128)(2,1)S(1)}, bf16[1152,768]{1,0:T(8,128)(2,1)}, u32[]{:S(2)}) copy-start(bf16[1152,768]{1,0:T(8,128)(2,1)} %get-tuple-element.31) | copy-start | bytes 5308420

commit v2 on v0

v2 whole, which is shorter than its diff:
```python
import functools

import jax
import jax.numpy as jnp
from jax import lax
from jax.experimental import pallas as pl
from jax.experimental.pallas import tpu as pltpu
from jax.sharding import PartitionSpec as P

AXES = ("grp", "loc")
BF = jnp.bfloat16
F32 = jnp.float32
E = 128
T = 128
K = 8
D = 2048
FF = 768
LANE = 128
SUB = 8
R8 = E * SUB
HALF = D // 2
HL = HALF // LANE
FOLD = D // SUB
FL = FOLD // LANE
GROUP = 4 * E
ROWS_A = GROUP + E
SEND_A = 2 * HALF + 2 * FOLD
SEND_B = 2 * HALF
BACK_A = HALF + FOLD
BACK_B = HALF + LANE
TN = 512
TF = 256
N1 = FF // TF
N2 = D // TN


def dot(a, b, ca=1, cb=0):
    return lax.dot_general(a, b, (((ca,), (cb,)), ((), ())), preferred_element_type=F32)


def cost(flops, bytes_accessed):
    return pl.CostEstimate(
        flops=int(flops), bytes_accessed=int(bytes_accessed), transcendentals=0
    )


ONE_DIM = pltpu.CompilerParams(dimension_semantics=("arbitrary",))
SINGLE = pl.Buffered(1)


def lanes(i):
    return slice(i * LANE, (i + 1) * LANE)


def halves(x, start, width):
    return jnp.concatenate(
        [x[:, start : start + width], x[:, HALF + start : HALF + start + width]], axis=0
    )


def pair_select(rank, weight, base):
    sub = lax.broadcasted_iota(jnp.int32, (E, SUB, T), 1)
    slot = (base + sub // 2).astype(F32)
    hit = jnp.where(rank[:, None, :] == slot, weight, 0.0)
    even = (sub % 2) == 0
    left = jnp.where(even, hit, 0.0).reshape(R8, T)
    right = jnp.where(even, 0.0, hit).reshape(R8, T)
    return jnp.concatenate([left, right], axis=1).astype(BF)


def pack_a_kernel(
    ids_hbm, gates_hbm, x_hbm, g_hbm, out_hbm, sel_hbm, sel9_hbm, rank_hbm, gate_hbm,
    ids_ref, gates_ref, x_ref, g_ref, sel_ref, sel9_ref, rank_ref, gate_ref,
    selg, fold, out, in_sems, out_sems,
):
    loads = [
        pltpu.make_async_copy(source, target, in_sems.at[n])
        for n, (source, target) in enumerate(
            (
                (ids_hbm, ids_ref),
                (gates_hbm, gates_ref),
                (x_hbm, x_ref),
                (g_hbm, g_ref),
            )
        )
    ]
    for load in loads:
        load.start()
    stores = []

    def send(source, target):
        store = pltpu.make_async_copy(source, target, out_sems.at[len(stores)])
        store.start()
        stores.append(store)

    def send_piece(piece):
        cols = pl.ds(piece * TN, TN)
        send(out.at[:, cols], out_hbm.at[:, cols])

    loads[0].wait()
    loads[1].wait()
    expert = lax.broadcasted_iota(jnp.int32, (E, T), 0)
    member = jnp.zeros((E, T), F32)
    gate = jnp.zeros((E, T), F32)
    for k in range(K):
        hit = ids_ref[k : k + 1, :] == expert
        member = jnp.where(hit, 1.0, member)
        gate = jnp.where(hit, gates_ref[k : k + 1, :].astype(F32), gate)
    earlier = (
        lax.broadcasted_iota(jnp.int32, (T, T), 0)
        < lax.broadcasted_iota(jnp.int32, (T, T), 1)
    ).astype(F32)
    rank = dot(member.astype(BF), earlier.astype(BF))
    rank = jnp.where(member > 0.0, rank, -1.0)
    rank_ref[...] = rank
    gate_ref[...] = gate
    sel9 = jnp.where(rank == float(SUB), 1.0, 0.0)
    sel9_ref[...] = sel9.astype(BF)
    sel9g = (sel9 * gate).astype(BF)
    sel_ref[...] = pair_select(rank, 1.0, 0)
    selg[...] = pair_select(rank, gate[:, None, :], 0)

    tiles = HALF // TN
    loads[2].wait()
    for c in range(tiles):
        out[:, c * TN : (c + 1) * TN] = dot(
            sel_ref[...], halves(x_ref, c * TN, TN)
        ).astype(BF)
        send_piece(c)
    loads[3].wait()
    for c in range(tiles):
        at = (tiles + 1 + c) * TN
        out[:, at : at + TN] = dot(selg[...], halves(g_ref, c * TN, TN)).astype(BF)
        send_piece(tiles + 1 + c)
    nine = dot(sel9_ref[...], x_ref[...])
    nine_g = dot(sel9g, g_ref[...])
    for i in range(SUB):
        rows = pl.ds(i, E, stride=SUB)
        for h in range(FL):
            at = i * FOLD + h * LANE
            fold[h, rows, :] = nine[:, at : at + LANE]
            fold[FL + h, rows, :] = nine_g[:, at : at + LANE]
    for h in range(2 * FL):
        at = HALF + h * LANE
        out[:, at : at + LANE] = fold[h].astype(BF)
    send_piece(tiles)
    send(sel_ref, sel_hbm)
    send(sel9_ref, sel9_hbm)
    send(rank_ref, rank_hbm)
    send(gate_ref, gate_hbm)
    for store in stores:
        store.wait()


def pack_a(ids_t, gates_t, acts, grad):
    return pl.pallas_call(
        pack_a_kernel,
        in_specs=[pl.BlockSpec(memory_space=pl.ANY)] * 4,
        out_specs=[pl.BlockSpec(memory_space=pl.ANY)] * 5,
        out_shape=[
            jax.ShapeDtypeStruct((R8, SEND_A), BF),
            jax.ShapeDtypeStruct((R8, 2 * T), BF),
            jax.ShapeDtypeStruct((E, T), BF),
            jax.ShapeDtypeStruct((E, T), F32),
            jax.ShapeDtypeStruct((E, T), F32),
        ],
        scratch_shapes=[
            pltpu.VMEM((K, T), jnp.int32),
            pltpu.VMEM((K, T), BF),
            pltpu.VMEM((T, D), BF),
            pltpu.VMEM((T, D), BF),
            pltpu.VMEM((R8, 2 * T), BF),
            pltpu.VMEM((E, T), BF),
            pltpu.VMEM((E, T), F32),
            pltpu.VMEM((E, T), F32),
            pltpu.VMEM((R8, 2 * T), BF),
            pltpu.VMEM((2 * FL, R8, LANE), F32),
            pltpu.VMEM((R8, SEND_A), BF),
            pltpu.SemaphoreType.DMA((4,)),
            pltpu.SemaphoreType.DMA((SEND_A // TN + 4,)),
        ],
        cost_estimate=cost(4 * R8 * T * D, 2 * R8 * SEND_A + 4 * T * D),
        name="pack_a",
    )(ids_t, gates_t, acts, grad)


def pack_b_kernel(rank_ref, gate_ref, x_ref, g_ref, out_ref, sel_t_ref, mix_ref, sel, selg):
    j = pl.program_id(0)
    tiles = HALF // TN

    @pl.when(j == 0)
    def _():
        rank = rank_ref[...]
        sel[...] = pair_select(rank, 1.0, 4)
        selg[...] = pair_select(rank, gate_ref[...][:, None, :], 4)
        sub = lax.broadcasted_iota(jnp.int32, (E, SUB, T), 1)
        slot = (sub // 2 + 4 * (sub % 2)).astype(F32)
        mix_ref[...] = jnp.where(rank[:, None, :] == slot, 1.0, 0.0).reshape(R8, T).astype(BF)

    @pl.when(j == 1)
    def _():
        sel_t_ref[...] = sel[...].T

    for c in range(tiles):

        @pl.when(j == c)
        def _():
            out_ref[...] = dot(sel[...], halves(x_ref, c * TN, TN)).astype(BF)

        @pl.when(j == tiles + c)
        def _():
            out_ref[...] = dot(selg[...], halves(g_ref, c * TN, TN)).astype(BF)


def pack_b(rank, gate, acts, grad):
    whole = lambda j: (0, 0)
    return pl.pallas_call(
        pack_b_kernel,
        grid=(SEND_B // TN,),
        in_specs=[
            pl.BlockSpec((E, T), whole),
            pl.BlockSpec((E, T), whole),
            pl.BlockSpec((T, D), whole),
            pl.BlockSpec((T, D), whole),
        ],
        out_specs=[
            pl.BlockSpec((R8, TN), lambda j: (0, j)),
            pl.BlockSpec((2 * T, R8), whole),
            pl.BlockSpec((R8, T), whole),
        ],
        out_shape=[
            jax.ShapeDtypeStruct((R8, SEND_B), BF),
            jax.ShapeDtypeStruct((2 * T, R8), BF),
            jax.ShapeDtypeStruct((R8, T), BF),
        ],
        scratch_shapes=[pltpu.VMEM((R8, 2 * T), BF), pltpu.VMEM((R8, 2 * T), BF)],
        compiler_params=ONE_DIM,
        cost_estimate=cost(4 * R8 * T * D, 2 * R8 * SEND_B + 4 * T * D),
        name="pack_b",
    )(rank, gate, acts, grad)


def expert_kernel(
    nine, y_ref, wg_ref, wu_ref, wd_ref, wg2_ref, wu2_ref, *rest
):
    if nine:
        out_ref, x_ref, g_ref, dpre_ref, dup_ref, hid_ref, tot_ref, fold, gsum = rest
    else:
        tot_ref, out_ref, x_ref, g_ref, dpre_ref, dup_ref, hid_ref, fold, gsum = rest
    i = pl.program_id(0)
    rows_all = GROUP + (E if nine else 0)
    step = rows_all // 2
    after = HALF + (2 * FOLD if nine else 0)

    def unfold(base, base9, rows_ref):
        for c in range(HL):
            at = base + c * LANE
            fold[c] = y_ref[:, at : at + LANE].astype(F32)
            for h in range(2):
                to = h * HALF + c * LANE
                rows_ref[0:GROUP, to : to + LANE] = fold[
                    c, pl.ds(h, GROUP, stride=2), :
                ].astype(BF)
        if nine:
            for h in range(FL):
                at = base9 + h * LANE
                fold[h] = y_ref[:, at : at + LANE].astype(F32)
            for s in range(SUB):
                for h in range(FL):
                    to = s * FOLD + h * LANE
                    rows_ref[GROUP:rows_all, to : to + LANE] = fold[
                        h, pl.ds(s, E, stride=SUB), :
                    ].astype(BF)

    @pl.when(i == 0)
    def _():
        unfold(0, HALF, x_ref)
        unfold(after, HALF + FOLD, g_ref)
        gsum[...] = jnp.zeros_like(gsum)

    @pl.when(i < N1)
    def _():
        cols = pl.ds(pl.multiple_of(jnp.minimum(i, N1 - 1) * TF, TF), TF)
        for m in range(2):
            rows = pl.ds(m * step, step)
            x = x_ref[rows, :]
            pre = dot(x, wg_ref[...])
            up = dot(x, wu_ref[...])
            dh = dot(g_ref[rows, :], wd_ref[...], 1, 1)
            s = jax.nn.sigmoid(pre)
            act = pre * s
            hid = act * up
            part = hid * dh
            gsum[rows, :] += part[:, 0:LANE] + part[:, LANE:TF]
            hid_ref[rows, cols] = hid.astype(BF)
            dup_ref[rows, cols] = (dh * act).astype(BF)
            dpre_ref[rows, cols] = (dh * up * s * (1.0 + pre * (1.0 - s))).astype(BF)

    @pl.when((i >= N1) & (i < N1 + N2))
    def _():
        j = i - N1
        half = j // 2
        for m in range(2):
            rows = pl.ds(m * step, step)
            dx = dot(dpre_ref[rows, :], wg2_ref[...], 1, 1)
            dx = dx + dot(dup_ref[rows, :], wu2_ref[...], 1, 1)
            keep = min(step, GROUP - m * step)
            for q in range(TN // LANE):
                fold[
                    (j % 2) * (TN // LANE) + q,
                    pl.ds(2 * m * step + half, keep, stride=2),
                    :,
                ] = dx[0:keep, lanes(q)]
            if keep < step:
                for q in range(TN // LANE):
                    fold[HL + q % FL, pl.ds(j * (TN // FOLD) + q // FL, E, stride=SUB), :] = dx[
                        keep:step, lanes(q)
                    ]

    @pl.when(i == N1 + N2)
    def _():
        for c in range(HL + (FL if nine else 0)):
            out_ref[:, lanes(c)] = fold[c].astype(BF)
        total = jnp.sum(gsum[...], axis=1, keepdims=True)
        total = jnp.broadcast_to(total, (rows_all, LANE))
        if nine:
            tot_ref[...] = total
        else:
            fold[0, pl.ds(0, GROUP, stride=2), :] = tot_ref[0:GROUP, :]
            fold[0, pl.ds(1, GROUP, stride=2), :] = total
            for s in range(SUB):
                fold[1, pl.ds(s, E, stride=SUB), :] = tot_ref[GROUP:ROWS_A, :]
            lane = lax.broadcasted_iota(jnp.int32, (R8, LANE), 1)
            out_ref[:, lanes(HL)] = jnp.where(lane == 1, fold[1], fold[0]).astype(BF)


def expert_side(nine, y, wg, wu, wd, *totals):
    rows_all = GROUP + (E if nine else 0)
    send, back = (SEND_A, BACK_A) if nine else (SEND_B, BACK_B)
    first = lambda i: (0, jnp.minimum(i, N1 - 1))
    second = lambda i: (jnp.clip(i - N1, 0, N2 - 1), 0)
    whole = lambda i: (0, 0)
    return pl.pallas_call(
        functools.partial(expert_kernel, nine),
        grid=(N1 + N2 + 1,),
        in_specs=[
            pl.BlockSpec((R8, send), whole, pipeline_mode=SINGLE),
            pl.BlockSpec((D, TF), first),
            pl.BlockSpec((D, TF), first),
            pl.BlockSpec((TF, D), lambda i: (jnp.minimum(i, N1 - 1), 0)),
            pl.BlockSpec((TN, FF), second),
            pl.BlockSpec((TN, FF), second),
        ]
        + [pl.BlockSpec((ROWS_A, LANE), whole) for _ in totals],
        out_specs=[
            pl.BlockSpec((R8, back), whole, pipeline_mode=SINGLE),
            pl.BlockSpec((rows_all, D), whole, pipeline_mode=SINGLE),
            pl.BlockSpec((rows_all, D), whole, pipeline_mode=SINGLE),
            pl.BlockSpec((rows_all, FF), whole, pipeline_mode=SINGLE),
            pl.BlockSpec((rows_all, FF), whole, pipeline_mode=SINGLE),
            pl.BlockSpec((rows_all, FF), whole, pipeline_mode=SINGLE),
        ]
        + [pl.BlockSpec((ROWS_A, LANE), whole)] * nine,
        out_shape=[
            jax.ShapeDtypeStruct((R8, back), BF),
            jax.ShapeDtypeStruct((rows_all, D), BF),
            jax.ShapeDtypeStruct((rows_all, D), BF),
            jax.ShapeDtypeStruct((rows_all, FF), BF),
            jax.ShapeDtypeStruct((rows_all, FF), BF),
            jax.ShapeDtypeStruct((rows_all, FF), BF),
        ]
        + [jax.ShapeDtypeStruct((ROWS_A, LANE), F32)] * nine,
        scratch_shapes=[
            pltpu.VMEM((HL + FL, R8, LANE), F32),
            pltpu.VMEM((rows_all, LANE), F32),
        ],
        compiler_params=ONE_DIM,
        cost_estimate=cost(10 * rows_all * D * FF, 40e6),
        name="expert_a" if nine else "expert_b",
    )(y, wg, wu, wd, wg, wu, *totals)


def combine_a_kernel(sel_ref, sel9_ref, y_ref, y9_ref, out_ref, fold, nine):
    j = pl.program_id(0)

    @pl.when(j == 0)
    def _():
        for h in range(FL):
            fold[h] = y9_ref[:, lanes(h)].astype(F32)
        for s in range(SUB):
            for h in range(FL):
                at = s * FOLD + h * LANE
                nine[:, at : at + LANE] = fold[h, pl.ds(s, E, stride=SUB), :].astype(BF)

    acc = dot(sel_ref[...], y_ref[...], 0, 0)
    cols = pl.ds(pl.multiple_of(j * TN, TN), TN)
    cols2 = pl.ds(pl.multiple_of(HALF + j * TN, TN), TN)
    out_ref[0:T, :] = acc[0:T] + dot(sel9_ref[...], nine[:, cols], 0, 0)
    out_ref[T : 2 * T, :] = acc[T : 2 * T] + dot(sel9_ref[...], nine[:, cols2], 0, 0)


def combine_a(sel, sel9, y):
    whole = lambda j: (0, 0)
    return pl.pallas_call(
        combine_a_kernel,
        grid=(HALF // TN,),
        in_specs=[
            pl.BlockSpec((R8, 2 * T), whole),
            pl.BlockSpec((E, T), whole),
            pl.BlockSpec((R8, TN), lambda j: (0, j)),
            pl.BlockSpec((R8, FOLD), lambda j: (0, HALF // FOLD)),
        ],
        out_specs=pl.BlockSpec((2 * T, TN), lambda j: (0, j)),
        out_shape=jax.ShapeDtypeStruct((2 * T, HALF), F32),
        scratch_shapes=[
            pltpu.VMEM((FL, R8, LANE), F32),
            pltpu.VMEM((E, D), BF),
        ],
        compiler_params=ONE_DIM,
        cost_estimate=cost(2 * R8 * T * D, 2 * R8 * BACK_A + 4 * T * D),
        name="combine_a",
    )(sel, sel9, y, y)


CN = 256


def combine_b_kernel(
    ids_hbm, gates_hbm, mix_hbm, sel9_hbm, sel_t_hbm, part_hbm, y_hbm, out_hbm, gg_hbm,
    ids_ref, gates_ref, mix_ref, sel9_ref, sel_t_ref, part_ref, y_ref, out_ref, gg_ref,
    fold, in_sems, out_sems,
):
    pieces = HALF // CN

    def load(n, source, target):
        copy = pltpu.make_async_copy(source, target, in_sems.at[n])
        copy.start()
        return copy

    gate_cols = pl.ds(HALF, LANE)
    first = [
        load(0, sel_t_hbm, sel_t_ref),
        load(1, part_hbm, part_ref),
    ]
    parts = []
    for p in range(pieces):
        cols = pl.ds(p * CN, CN)
        parts.append(load(2 + p, y_hbm.at[:, cols], y_ref.at[:, cols]))
    rest = [
        load(2 + pieces, y_hbm.at[:, gate_cols], y_ref.at[:, gate_cols]),
        load(3 + pieces, mix_hbm, mix_ref),
        load(4 + pieces, sel9_hbm, sel9_ref),
        load(5 + pieces, ids_hbm, ids_ref),
        load(6 + pieces, gates_hbm, gates_ref),
    ]
    stores = []

    def send(source, target):
        store = pltpu.make_async_copy(source, target, out_sems.at[len(stores)])
        store.start()
        stores.append(store)

    for copy in first:
        copy.wait()
    for p in range(pieces):
        parts[p].wait()
        at = p * CN
        acc = part_ref[:, at : at + CN] + dot(sel_t_ref[...], y_ref[:, at : at + CN])
        out_ref[:, at : at + CN] = acc[0:T].astype(BF)
        out_ref[:, HALF + at : HALF + at + CN] = acc[T : 2 * T].astype(BF)
    send(out_ref, out_hbm)
    for copy in rest:
        copy.wait()
    fold[...] = y_ref[:, HALF:BACK_B].astype(F32)
    own = jnp.broadcast_to(fold[:, 0:1], (R8, T))
    picked = jnp.where(mix_ref[...].astype(F32) > 0.0, own, 0.0).reshape(E, SUB, T)
    ninth = jnp.broadcast_to(fold[pl.ds(0, E, stride=SUB), :][:, 1:2], (E, T))
    table = jnp.sum(picked, axis=1)
    table = table + jnp.where(sel9_ref[...].astype(F32) > 0.0, ninth, 0.0)
    expert = lax.broadcasted_iota(jnp.int32, (E, T), 0)
    totals = []
    for k in range(K):
        hit = ids_ref[k : k + 1, :] == expert
        totals.append(jnp.sum(jnp.where(hit, table, 0.0), axis=0, keepdims=True))
    total = jnp.concatenate(totals, axis=0) / gates_ref[...].astype(F32)
    gg_ref[...] = total.astype(BF)
    send(gg_ref, gg_hbm)
    for store in stores:
        store.wait()


def combine_b(ids_t, gates_t, mix, sel9, sel_t, part, y):
    return pl.pallas_call(
        combine_b_kernel,
        in_specs=[pl.BlockSpec(memory_space=pl.ANY)] * 7,
        out_specs=[pl.BlockSpec(memory_space=pl.ANY)] * 2,
        out_shape=[
            jax.ShapeDtypeStruct((T, D), BF),
            jax.ShapeDtypeStruct((K, T), BF),
        ],
        scratch_shapes=[
            pltpu.VMEM((K, T), jnp.int32),
            pltpu.VMEM((K, T), BF),
            pltpu.VMEM((R8, T), BF),
            pltpu.VMEM((E, T), BF),
            pltpu.VMEM((2 * T, R8), BF),
            pltpu.VMEM((2 * T, HALF), F32),
            pltpu.VMEM((R8, BACK_B), BF),
            pltpu.VMEM((T, D), BF),
            pltpu.VMEM((K, T), BF),
            pltpu.VMEM((R8, LANE), F32),
            pltpu.SemaphoreType.DMA((7 + HALF // CN,)),
            pltpu.SemaphoreType.DMA((2,)),
        ],
        cost_estimate=cost(2 * R8 * T * D, 2 * R8 * BACK_B + 4 * T * D),
        name="combine_b",
    )(ids_t, gates_t, mix, sel9, sel_t, part, y)


def exchange(x):
    width = x.shape[1]
    y = lax.all_to_all(
        x.reshape(E, SUB, width), AXES, split_axis=0, concat_axis=0, tiled=True
    )
    return y.reshape(R8, width)


def body(acts, out_grad, expert_ids, gate_vals, w_gate, w_up, w_down):
    ids_t = expert_ids.T
    gates_t = gate_vals.T
    wg, wu, wd = w_gate[0], w_up[0], w_down[0]
    send_a, sel_a, sel9, rank, gate = pack_a(ids_t, gates_t, acts, out_grad)
    got_a = exchange(send_a)
    send_b, sel_b_t, mix = pack_b(rank, gate, acts, out_grad)
    got_b = exchange(send_b)
    back_a, x_a, g_a, dpre_a, dup_a, hid_a, totals = expert_side(True, got_a, wg, wu, wd)
    wg_part = dot(x_a, dpre_a, 0, 0)
    wd_part = dot(hid_a, g_a, 0, 0)
    back_a, wg_part, wd_part = lax.optimization_barrier((back_a, wg_part, wd_part))
    home_a = exchange(back_a)
    back_b, x_b, g_b, dpre_b, dup_b, hid_b = expert_side(False, got_b, wg, wu, wd, totals)
    home_b = exchange(back_b)
    wg_grad = (wg_part + dot(x_b, dpre_b, 0, 0)).astype(BF)
    wu_grad = (dot(x_a, dup_a, 0, 0) + dot(x_b, dup_b, 0, 0)).astype(BF)
    wd_grad = (wd_part + dot(hid_b, g_b, 0, 0)).astype(BF)
    part = combine_a(sel_a, sel9, home_a)
    grad_acts, gate_grad_t = combine_b(ids_t, gates_t, mix, sel9, sel_b_t, part, home_b)
    return (
        grad_acts,
        gate_grad_t.T,
        wg_grad[None],
        wu_grad[None],
        wd_grad[None],
    )


def solution(mesh):
    rows = P(AXES, None)
    mats = P(AXES, None, None)
    return jax.shard_map(
        body,
        mesh=mesh,
        in_specs=(rows, rows, rows, rows, mats, mats, mats),
        out_specs=(rows, rows, mats, mats, mats),
        check_vma=False,
    )
```

time: 465 us -> 223 us (0.48)
  waiting for transfers between devices: 224 us -> 88.8 us
  local copies, waits for them, and re-layouts: 114 us -> 0.04 us
  Pallas kernels: 0 us -> 63 us
  matrix products: 61.1 us -> 30.8 us
  starting transfers between devices: 48 us -> 35.1 us
  other arithmetic: 8.8 us -> 0.01 us
    all_to_all x5 -> x4, waiting for transfers between devices: 224 us -> 88.8 us  [exchange(): lax.all_to_all(x.reshape(E, SUB, width), AXES, split_axis=0, concat_axis=...]
    pallas_call x0 -> x6, Pallas kernels: none -> 63 us  [the longest x2 45.3 us: expert_side(): pl.pallas_call(functools.partial(expert_kernel, nine), grid=(N1 + N2 + 1,...]
    all_to_all x8 -> x0, local copies, waits for them, and re-layouts: 50.9 us -> none  [the longest x2 16.7 us: body(): lax.all_to_all(send_grad, ('grp', 'loc'), split_axis=0, concat_axis=0, ti...]
    gather x5 -> x0, local copies, waits for them, and re-layouts: 49.6 us -> none  [the longest x1 11.9 us: body(): back_rows[slot_of].reshape(tokens, top_count, width).astype(jnp.float32)]
    dot_general x8 -> x6, matrix products: 61.1 us -> 30.8 us  [dot(): lax.dot_general(a, b, (((ca,), (cb,)), ((), ())), preferred_element_type=...]
    all_to_all x5 -> x4, starting transfers between devices: 48 us -> 35.1 us  [exchange(): lax.all_to_all(x.reshape(E, SUB, width), AXES, split_axis=0, concat_axis=...]
    reduce_sum x2 -> x0, other arithmetic: 6.24 us -> none  [the longest x1 5.88 us: body(): grad_acts = jnp.sum(picked, axis=1).astype(jnp.bfloat16)]
  transfers between devices with their start and end apart: 5 -> 4, of which waited for: 3 -> 4; matrix products, arithmetic and copies ran while one was open for 18% -> 14% of each run, Pallas kernels for 0% -> 25%
where the time goes in v2:
time: 223 us; the launch traced here: 219 us
  waiting for transfers between devices  88.8 us (40%)
  Pallas kernels  63 us (28%)
  starting transfers between devices  35.1 us (16%)
  matrix products  30.8 us (14%)
    all_to_all x4, waiting for transfers between devices, exchange(): lax.all_to_all(x.reshape(E, SUB, width), AXES, split_axis=0, concat_axis=...  88.8 us
    pallas_call x2, Pallas kernels, expert_side(): pl.pallas_call(functools.partial(expert_kernel, nine), grid=(N1 + N2 + 1,...  45.3 us
    all_to_all x4, starting transfers between devices, exchange(): lax.all_to_all(x.reshape(E, SUB, width), AXES, split_axis=0, concat_axis=...  35.1 us
    dot_general x6, matrix products, dot(): lax.dot_general(a, b, (((ca,), (cb,)), ((), ())), preferred_element_type=...  30.8 us
    pallas_call x1, Pallas kernels, pack_b(): pl.pallas_call(pack_b_kernel, grid=(SEND_B // TN,), in_specs=[pl.BlockSpe...  5.5 us
  transfers between devices with their start and end apart: 4, of which 4 were waited for; matrix products, arithmetic and copies ran while one was open for 14% of the time, Pallas kernels for 25%

profile of v2, /device:TPU:13, one launch (start us, length us, event | category | flops | bytes accessed | tf_op | source)
XLA Modules:
  0.0 218.8 jit_solution(7603739235035491985)
XLA Ops:
  0.6 4.3 %pack_a.1 = (bf16[1024,2560]{1,0:T(8,128)(2,1)}, bf16[1024,256]{1,0:T(8,128)(2,1)}, bf16[128,128]{1,0:T(8,128)(2,1)}, f32[128,128]{1,0:T(8,128)}, f32[128,128]{1,0:T(8,128)}) custom-call(s32[8,128]{1,0:T(8,128)} %bitcast.40, bf16[8,128]{1,0:T(8,128)(2,1)} %bitcast.42, bf16[128,2048]{1,0:T(8,128)(2,1)} %x_ref.1, bf16[128,2048]{1,0:T(8,128)(2,1)} %g_ref.1), custom_call_target="tpu_custom_call" | custom-call | flops 1073741824 | bytes 6291456 | tf_op jit(solution)/shard_map/pack_a/pallas_call | solution.py:156
  4.9 11.1 %all-to-all-start = ((bf16[128,8,2560]{2,1,0:T(8,128)(2,1)}), bf16[128,8,2560]{2,1,0:T(8,128)(2,1)}, u32[]{:S(2)}, u32[]{:S(2)}) async-start(bf16[128,8,2560]{2,1,0:T(8,128)(2,1)} %bitcast.36), calls=%async_computation | async-start | bytes 10485760 | tf_op jit(solution)/shard_map/all_to_all | solution.py:522
  16.0 5.5 %pack_b.1 = (bf16[1024,2048]{1,0:T(8,128)(2,1)}, bf16[256,1024]{1,0:T(8,128)(2,1)}, bf16[1024,128]{1,0:T(8,128)(2,1)}) custom-call(f32[128,128]{1,0:T(8,128)} %get-tuple-element.31.rank_ref, f32[128,128]{1,0:T(8,128)} %get-tuple-element.32.gate_ref, bf16[128,2048]{1,0:T(8,128)(2,1)} %x_ref.1, bf16[128,2048]{1,0:T(8,128)(2,1)} %g_ref.1), custom_call_target="tpu_custom_call" | custom-call | flops 1073741824 | bytes 5242880 | tf_op jit(solution)/shard_map/pack_b/pallas_call | solution.py:217
  21.5 56.0 %all-to-all-done = bf16[128,8,2560]{2,1,0:T(8,128)(2,1)} async-done(((bf16[128,8,2560]{2,1,0:T(8,128)(2,1)}), bf16[128,8,2560]{2,1,0:T(8,128)(2,1)}, u32[]{:S(2)}, u32[]{:S(2)}) %all-to-all-start) | async-done | bytes 5242912 | tf_op jit(solution)/shard_map/all_to_all | solution.py:522
  77.5 8.1 %all-to-all-start.2 = ((bf16[128,8,2048]{2,1,0:T(8,128)(2,1)}), bf16[128,8,2048]{2,1,0:T(8,128)(2,1)}, u32[]{:S(2)}, u32[]{:S(2)}) async-start(bf16[128,8,2048]{2,1,0:T(8,128)(2,1)} %bitcast.37), calls=%async_computation.2 | async-start | bytes 8388608 | tf_op jit(solution)/shard_map/all_to_all | solution.py:522
  85.6 24.1 %expert_a.1 = (bf16[1024,1280]{1,0:T(8,128)(2,1)}, bf16[640,2048]{1,0:T(8,128)(2,1)}, bf16[640,2048]{1,0:T(8,128)(2,1)}, bf16[640,768]{1,0:T(8,128)(2,1)}, bf16[...) custom-call(bf16[1024,2560]{1,0:T(8,128)(2,1)} %bitcast.3.y_ref, bf16[2048,768]{1,0:T(8,128)(2,1)} %bitcast.44, ...), custom_call_target="tpu_custom_call" | custom-call | flops 10066329600 | bytes 40000000 | tf_op jit(solution)/shard_map/expert_a/pallas_call | solution.py:343
  109.7 7.5 %fusion.3 = f32[2048,768]{1,0:T(8,128)} fusion(bf16[640,2048]{1,0:T(8,128)(2,1)} %get-tuple-element.39, bf16[640,768]{1,0:T(8,128)(2,1)} %get-tuple-element.40), kind=kOutput, calls=%fused_computation.6 | convolution fusion | flops 2013265920 | bytes 9895936 | tf_op jit(solution)/shard_map/dot_general | solution.py:38
  117.1 0.0 copy-done.1
  117.1 0.0 copy-done.2
  117.1 4.6 %fusion.4 = f32[768,2048]{1,0:T(8,128)} fusion(bf16[640,768]{1,0:T(8,128)(2,1)S(1)} %copy-done.2, bf16[640,2048]{1,0:T(8,128)(2,1)S(1)} %copy-done.1), kind=kOutput, calls=%fused_computation.7 | convolution fusion | flops 2013265920 | bytes 9895936 | tf_op jit(solution)/shard_map/dot_general | solution.py:38
  121.8 13.9 %all-to-all-done.2 = bf16[128,8,2048]{2,1,0:T(8,128)(2,1)} async-done(((bf16[128,8,2048]{2,1,0:T(8,128)(2,1)}), bf16[128,8,2048]{2,1,0:T(8,128)(2,1)}, u32[]{:S(2)}, u32[]{:S(2)}) %all-to-all-start.2) | async-done | bytes 4194336 | tf_op jit(solution)/shard_map/all_to_all | solution.py:522
  135.6 7.2 %all-to-all-start.1 = ((bf16[128,8,1280]{2,1,0:T(8,128)(2,1)}), bf16[128,8,1280]{2,1,0:T(8,128)(2,1)S(1)}, u32[]{:S(2)}, u32[]{:S(2)}) async-start(bf16[128,8,1280]{2,1,0:T(8,128)(2,1)} %bitcast.38), calls=%async_computation.1 | async-start | bytes 5242880 | tf_op jit(solution)/shard_map/all_to_all | solution.py:522
  142.8 21.3 %expert_b.1 = (bf16[1024,1152]{1,0:T(8,128)(2,1)}, bf16[512,2048]{1,0:T(8,128)(2,1)}, bf16[512,2048]{1,0:T(8,128)(2,1)}, bf16[512,768]{1,0:T(8,128)(2,1)}, bf16[...) custom-call(bf16[1024,2048]{1,0:T(8,128)(2,1)} %bitcast.10.y_ref, bf16[2048,768]{1,0:T(8,128)(2,1)} %bitcast.46, ...), custom_call_target="tpu_custom_call" | custom-call | flops 8053063680 | bytes 40000000 | tf_op jit(solution)/shard_map/expert_b/pallas_call | solution.py:343
  164.1 11.7 %all-to-all-done.1 = bf16[128,8,1280]{2,1,0:T(8,128)(2,1)S(1)} async-done(((bf16[128,8,1280]{2,1,0:T(8,128)(2,1)}), bf16[128,8,1280]{2,1,0:T(8,128)(2,1)S(1)}, u32[]{:S(2)}, u32[]{:S(2)}) %all-to-all-start.1) | async-done | bytes 2621472 | tf_op jit(solution)/shard_map/all_to_all | solution.py:522
  175.8 8.7 %all-to-all-start.3 = ((bf16[128,8,1152]{2,1,0:T(8,128)(2,1)}), bf16[128,8,1152]{2,1,0:T(8,128)(2,1)}, u32[]{:S(2)}, u32[]{:S(2)}) async-start(bf16[128,8,1152]{2,1,0:T(8,128)(2,1)} %bitcast.39), calls=%async_computation.3 | async-start | bytes 4718592 | tf_op jit(solution)/shard_map/all_to_all | solution.py:522
  184.5 0.0 copy-start.3
  184.5 0.0 copy-start.6
  184.5 4.9 %fusion.5 = f32[2048,768]{1,0:T(8,128)S(1)} fusion(bf16[640,2048]{1,0:T(8,128)(2,1)} %get-tuple-element.39, bf16[640,768]{1,0:T(8,128)(2,1)} %get-tuple-element.52), kind=kOutput, calls=%fused_computation.8 | convolution fusion | flops 2013265920 | bytes 9895936 | tf_op jit(solution)/shard_map/dot_general | solution.py:38
  189.4 0.0 copy-done
  189.4 0.0 copy-done.3
  189.4 0.0 copy-done.6
  189.4 0.0 copy-start.5
  189.4 0.0 slice-start
  189.5 6.5 %fusion = bf16[1,2048,768]{2,1,0:T(8,128)(2,1)} fusion(f32[2048,768]{1,0:T(8,128)} %fusion.3, bf16[512,2048]{1,0:T(8,128)(2,1)S(1)} %copy-done.3, bf16[512,768]{1,0:T(8,128)(2,1)S(1)} %copy-done.6), kind=kOutput, calls=%fused_computation.3 | convolution fusion | flops 1613758464 | bytes 12320768 | tf_op jit(solution)/shard_map/dot_general | solution.py:38
  195.9 0.0 copy-done.5
  195.9 3.7 %fusion.1 = bf16[1,2048,768]{2,1,0:T(8,128)(2,1)} fusion(f32[2048,768]{1,0:T(8,128)S(1)} %fusion.5, bf16[512,2048]{1,0:T(8,128)(2,1)S(1)} %copy-done.3, bf16[512,768]{1,0:T(8,128)(2,1)S(1)} %copy-done.5), kind=kOutput, calls=%fused_computation.4 | convolution fusion | flops 1613758464 | bytes 12320768 | tf_op jit(solution)/shard_map/dot_general | solution.py:38
  199.7 0.0 slice-done
  199.7 0.0 copy-done.4
  199.7 3.7 %fusion.2 = bf16[1,768,2048]{2,1,0:T(8,128)(2,1)} fusion(f32[768,2048]{1,0:T(8,128)S(1)} %bitcast.35, bf16[512,768]{1,0:T(8,128)(2,1)S(1)} %copy-done.7, bf16[512,2048]{1,0:T(8,128)(2,1)S(1)} %copy-done.4), kind=kOutput, calls=%fused_computation.5 | convolution fusion | flops 1613758464 | bytes 12320768 | tf_op jit(solution)/shard_map/dot_general | solution.py:38
  203.4 3.7 %combine_a.1.part_hbm = f32[256,1024]{1,0:T(8,128)} custom-call(bf16[1024,256]{1,0:T(8,128)(2,1)} %get-tuple-element.36.sel_ref, bf16[128,128]{1,0:T(8,128)(2,1)} %get-tuple-element.34.sel9_ref.sel9_hbm, bf16[1024,1280]{1,0:T(8,128)(2,1)} %bitcast.32, bf16[1024,1280]{1,0:T(8,128)(2,1)} %bitcast.33), custom_call_target="tpu_custom_call" | custom-call | flops 536870912 | bytes 3670016 | tf_op jit(solution)/shard_map/combine_a/pallas_call | solution.py:404
  207.1 7.3 %all-to-all-done.3 = bf16[128,8,1152]{2,1,0:T(8,128)(2,1)} async-done(((bf16[128,8,1152]{2,1,0:T(8,128)(2,1)}), bf16[128,8,1152]{2,1,0:T(8,128)(2,1)}, u32[]{:S(2)}, u32[]{:S(2)}) %all-to-all-start.3) | async-done | bytes 2359328 | tf_op jit(solution)/shard_map/all_to_all | solution.py:522
  214.4 4.2 %combine_b.1 = (bf16[128,2048]{1,0:T(8,128)(2,1)}, bf16[8,128]{1,0:T(8,128)(2,1)}) custom-call(s32[8,128]{1,0:T(8,128)} %bitcast.41, bf16[8,128]{1,0:T(8,128)(2,1)} %bitcast.43, bf16[1024,128]{1,0:T(8,128)(2,1)} %get-tuple-element.33.mix_hbm, bf16[128,128]{1,0:T(8,128)(2,1)} %get-tuple-element.34.sel9_ref.sel9_hbm, ...), custom_call_target="tpu_custom_call" | custom-call | flops 536870912 | bytes 3407872 | tf_op jit(solution)/shard_map/combine_b/pallas_call | solution.py:493
  (9 shorter events, 0.0 us)
Async XLA Ops:
  4.9 72.6 %all-to-all-start = ((bf16[128,8,2560]{2,1,0:T(8,128)(2,1)}), bf16[128,8,2560]{2,1,0:T(8,128)(2,1)}, u32[]{:S(2)}, u32[]{:S(2)}) async-start(bf16[128,8,2560]{2,1,0:T(8,128)(2,1)} %bitcast.36), calls=%async_computation | async-start | bytes 10485760 | tf_op jit(solution)/shard_map/all_to_all | solution.py:522
  77.5 58.2 %all-to-all-start.2 = ((bf16[128,8,2048]{2,1,0:T(8,128)(2,1)}), bf16[128,8,2048]{2,1,0:T(8,128)(2,1)}, u32[]{:S(2)}, u32[]{:S(2)}) async-start(bf16[128,8,2048]{2,1,0:T(8,128)(2,1)} %bitcast.37), calls=%async_computation.2 | async-start | bytes 8388608 | tf_op jit(solution)/shard_map/all_to_all | solution.py:522
  109.7 7.5 %copy-start.1 = (bf16[640,2048]{1,0:T(8,128)(2,1)S(1)}, bf16[640,2048]{1,0:T(8,128)(2,1)}, u32[]{:S(2)}) copy-start(bf16[640,2048]{1,0:T(8,128)(2,1)} %get-tuple-element.42) | copy-start | bytes 7864324
  109.7 7.5 %copy-start.2 = (bf16[640,768]{1,0:T(8,128)(2,1)S(1)}, bf16[640,768]{1,0:T(8,128)(2,1)}, u32[]{:S(2)}) copy-start(bf16[640,768]{1,0:T(8,128)(2,1)} %get-tuple-element.41) | copy-start | bytes 2949124
  135.6 40.1 %all-to-all-start.1 = ((bf16[128,8,1280]{2,1,0:T(8,128)(2,1)}), bf16[128,8,1280]{2,1,0:T(8,128)(2,1)S(1)}, u32[]{:S(2)}, u32[]{:S(2)}) async-start(bf16[128,8,1280]{2,1,0:T(8,128)(2,1)} %bitcast.38), calls=%async_computation.1 | async-start | bytes 5242880 | tf_op jit(solution)/shard_map/all_to_all | solution.py:522
  175.8 13.6 %copy-start = (bf16[128,8,1280]{2,1,0:T(8,128)(2,1)}, bf16[128,8,1280]{2,1,0:T(8,128)(2,1)S(1)}, u32[]{:S(2)}) copy-start(bf16[128,8,1280]{2,1,0:T(8,128)(2,1)S(1)} %all-to-all-done.1) | copy-start | bytes 7864324
  175.8 38.6 %all-to-all-start.3 = ((bf16[128,8,1152]{2,1,0:T(8,128)(2,1)}), bf16[128,8,1152]{2,1,0:T(8,128)(2,1)}, u32[]{:S(2)}, u32[]{:S(2)}) async-start(bf16[128,8,1152]{2,1,0:T(8,128)(2,1)} %bitcast.39), calls=%async_computation.3 | async-start | bytes 4718592 | tf_op jit(solution)/shard_map/all_to_all | solution.py:522
  184.5 4.9 %copy-start.3 = (bf16[512,2048]{1,0:T(8,128)(2,1)S(1)}, bf16[512,2048]{1,0:T(8,128)(2,1)}, u32[]{:S(2)}) copy-start(bf16[512,2048]{1,0:T(8,128)(2,1)} %get-tuple-element.50) | copy-start | bytes 6291460
  184.5 4.9 %copy-start.6 = (bf16[512,768]{1,0:T(8,128)(2,1)S(1)}, bf16[512,768]{1,0:T(8,128)(2,1)}, u32[]{:S(2)}) copy-start(bf16[512,768]{1,0:T(8,128)(2,1)} %get-tuple-element.51) | copy-start | bytes 2359300
  189.4 6.5 %copy-start.5 = (bf16[512,768]{1,0:T(8,128)(2,1)S(1)}, bf16[512,768]{1,0:T(8,128)(2,1)}, u32[]{:S(2)}) copy-start(bf16[512,768]{1,0:T(8,128)(2,1)} %get-tuple-element.53) | copy-start | bytes 2359300
  189.4 10.2 %slice-start = ((s8[6291456]{0:T(1024)(128)(4,1)}), s8[4194304]{0:T(1024)(128)(4,1)S(1)}, s32[]{:S(2)}) async-start(s8[6291456]{0:T(1024)(128)(4,1)} %bitcast.34), calls=%async_computation.4 | async-start | bytes 8388608
  195.9 3.7 %slice-start.1 = ((s8[6291456]{0:T(1024)(128)(4,1)}), s8[2097152]{0:T(1024)(128)(4,1)S(1)}, s32[]{:S(2)}) async-start(s8[6291456]{0:T(1024)(128)(4,1)} %bitcast.34), calls=%async_computation.5 | async-start | bytes 4194304
  195.9 3.7 %copy-start.4 = (bf16[512,2048]{1,0:T(8,128)(2,1)S(1)}, bf16[512,2048]{1,0:T(8,128)(2,1)}, u32[]{:S(2)}) copy-start(bf16[512,2048]{1,0:T(8,128)(2,1)} %get-tuple-element.56) | copy-start | bytes 6291460
  195.9 3.7 %copy-start.7 = (bf16[512,768]{1,0:T(8,128)(2,1)S(1)}, bf16[512,768]{1,0:T(8,128)(2,1)}, u32[]{:S(2)}) copy-start(bf16[512,768]{1,0:T(8,128)(2,1)} %get-tuple-element.55) | copy-start | bytes 2359300

commit v3 on v2

--- a/solution.py
+++ b/solution.py
@@ -422,7 +422,7 @@
     )(sel, sel9, y, y)
 
 
-CN = 256
+CN = 512
 
 
 def combine_b_kernel(
@@ -431,28 +431,31 @@
     fold, in_sems, out_sems,
 ):
     pieces = HALF // CN
-
-    def load(n, source, target):
-        copy = pltpu.make_async_copy(source, target, in_sems.at[n])
+    count = iter(range(7 + 2 * pieces))
+
+    def load(source, target):
+        copy = pltpu.make_async_copy(source, target, in_sems.at[next(count)])
         copy.start()
         return copy
 
     gate_cols = pl.ds(HALF, LANE)
-    first = [
-        load(0, sel_t_hbm, sel_t_ref),
-        load(1, part_hbm, part_ref),
+    small = [
+        load(ids_hbm, ids_ref),
+        load(gates_hbm, gates_ref),
+        load(sel9_hbm, sel9_ref),
+        load(y_hbm.at[:, gate_cols], y_ref.at[:, gate_cols]),
+        load(mix_hbm, mix_ref),
     ]
+    first = load(sel_t_hbm, sel_t_ref)
     parts = []
     for p in range(pieces):
         cols = pl.ds(p * CN, CN)
-        parts.append(load(2 + p, y_hbm.at[:, cols], y_ref.at[:, cols]))
-    rest = [
-        load(2 + pieces, y_hbm.at[:, gate_cols], y_ref.at[:, gate_cols]),
-        load(3 + pieces, mix_hbm, mix_ref),
-        load(4 + pieces, sel9_hbm, sel9_ref),
-        load(5 + pieces, ids_hbm, ids_ref),
-        load(6 + pieces, gates_hbm, gates_ref),
-    ]
+        parts.append(
+            [
+                load(y_hbm.at[:, cols], y_ref.at[:, cols]),
+                load(part_hbm.at[:, cols], part_ref.at[:, cols]),
+            ]
+        )
     stores = []
 
     def send(source, target):
@@ -460,16 +463,7 @@
         store.start()
         stores.append(store)
 
-    for copy in first:
-        copy.wait()
-    for p in range(pieces):
-        parts[p].wait()
-        at = p * CN
-        acc = part_ref[:, at : at + CN] + dot(sel_t_ref[...], y_ref[:, at : at + CN])
-        out_ref[:, at : at + CN] = acc[0:T].astype(BF)
-        out_ref[:, HALF + at : HALF + at + CN] = acc[T : 2 * T].astype(BF)
-    send(out_ref, out_hbm)
-    for copy in rest:
+    for copy in small:
         copy.wait()
     fold[...] = y_ref[:, HALF:BACK_B].astype(F32)
     own = jnp.broadcast_to(fold[:, 0:1], (R8, T))
@@ -485,6 +479,17 @@
     total = jnp.concatenate(totals, axis=0) / gates_ref[...].astype(F32)
     gg_ref[...] = total.astype(BF)
     send(gg_ref, gg_hbm)
+    first.wait()
+    for p in range(pieces):
+        for copy in parts[p]:
+            copy.wait()
+        at = p * CN
+        acc = part_ref[:, at : at + CN] + dot(sel_t_ref[...], y_ref[:, at : at + CN])
+        out_ref[:, at : at + CN] = acc[0:T].astype(BF)
+        out_ref[:, HALF + at : HALF + at + CN] = acc[T : 2 * T].astype(BF)
+        for start in (at, HALF + at):
+            cols = pl.ds(start, CN)
+            send(out_ref.at[:, cols], out_hbm.at[:, cols])
     for store in stores:
         store.wait()
 
@@ -509,8 +514,8 @@
             pltpu.VMEM((T, D), BF),
             pltpu.VMEM((K, T), BF),
             pltpu.VMEM((R8, LANE), F32),
-            pltpu.SemaphoreType.DMA((7 + HALF // CN,)),
-            pltpu.SemaphoreType.DMA((2,)),
+            pltpu.SemaphoreType.DMA((7 + 2 * HALF // CN,)),
+            pltpu.SemaphoreType.DMA((1 + 2 * HALF // CN,)),
         ],
         cost_estimate=cost(2 * R8 * T * D, 2 * R8 * BACK_B + 4 * T * D),
         name="combine_b",

time: 223 us -> 222 us (level)
  no operation moved by 1% of the time
where the time goes in v3:
time: 222 us; the launch traced here: 218 us
  waiting for transfers between devices  88.8 us (40%)
  Pallas kernels  62.3 us (28%)
  starting transfers between devices  35.1 us (16%)
  matrix products  30.8 us (14%)
    all_to_all x4, waiting for transfers between devices, exchange(): lax.all_to_all(x.reshape(E, SUB, width), AXES, split_axis=0, concat_axis=...  88.8 us
    pallas_call x2, Pallas kernels, expert_side(): pl.pallas_call(functools.partial(expert_kernel, nine), grid=(N1 + N2 + 1,...  45.3 us
    all_to_all x4, starting transfers between devices, exchange(): lax.all_to_all(x.reshape(E, SUB, width), AXES, split_axis=0, concat_axis=...  35.1 us
    dot_general x6, matrix products, dot(): lax.dot_general(a, b, (((ca,), (cb,)), ((), ())), preferred_element_type=...  30.8 us
    pallas_call x1, Pallas kernels, pack_b(): pl.pallas_call(pack_b_kernel, grid=(SEND_B // TN,), in_specs=[pl.BlockSpe...  5.5 us
  transfers between devices with their start and end apart: 4, of which 4 were waited for; matrix products, arithmetic and copies ran while one was open for 14% of the time, Pallas kernels for 25%

profile of v3, /device:TPU:13, one launch (start us, length us, event | category | flops | bytes accessed | tf_op | source)
XLA Modules:
  0.0 218.1 jit_solution(17187117336748294131)
XLA Ops:
  0.6 4.3 %pack_a.1 = (bf16[1024,2560]{1,0:T(8,128)(2,1)}, bf16[1024,256]{1,0:T(8,128)(2,1)}, bf16[128,128]{1,0:T(8,128)(2,1)}, f32[128,128]{1,0:T(8,128)}, f32[128,128]{1,0:T(8,128)}) custom-call(s32[8,128]{1,0:T(8,128)} %bitcast.40, bf16[8,128]{1,0:T(8,128)(2,1)} %bitcast.42, bf16[128,2048]{1,0:T(8,128)(2,1)} %x_ref.1, bf16[128,2048]{1,0:T(8,128)(2,1)} %g_ref.1), custom_call_target="tpu_custom_call" | custom-call | flops 1073741824 | bytes 6291456 | tf_op jit(solution)/shard_map/pack_a/pallas_call | solution.py:156
  4.9 11.1 %all-to-all-start = ((bf16[128,8,2560]{2,1,0:T(8,128)(2,1)}), bf16[128,8,2560]{2,1,0:T(8,128)(2,1)}, u32[]{:S(2)}, u32[]{:S(2)}) async-start(bf16[128,8,2560]{2,1,0:T(8,128)(2,1)} %bitcast.36), calls=%async_computation | async-start | bytes 10485760 | tf_op jit(solution)/shard_map/all_to_all | solution.py:527
  16.0 5.5 %pack_b.1 = (bf16[1024,2048]{1,0:T(8,128)(2,1)}, bf16[256,1024]{1,0:T(8,128)(2,1)}, bf16[1024,128]{1,0:T(8,128)(2,1)}) custom-call(f32[128,128]{1,0:T(8,128)} %get-tuple-element.31.rank_ref, f32[128,128]{1,0:T(8,128)} %get-tuple-element.32.gate_ref, bf16[128,2048]{1,0:T(8,128)(2,1)} %x_ref.1, bf16[128,2048]{1,0:T(8,128)(2,1)} %g_ref.1), custom_call_target="tpu_custom_call" | custom-call | flops 1073741824 | bytes 5242880 | tf_op jit(solution)/shard_map/pack_b/pallas_call | solution.py:217
  21.5 56.0 %all-to-all-done = bf16[128,8,2560]{2,1,0:T(8,128)(2,1)} async-done(((bf16[128,8,2560]{2,1,0:T(8,128)(2,1)}), bf16[128,8,2560]{2,1,0:T(8,128)(2,1)}, u32[]{:S(2)}, u32[]{:S(2)}) %all-to-all-start) | async-done | bytes 5242912 | tf_op jit(solution)/shard_map/all_to_all | solution.py:527
  77.5 8.1 %all-to-all-start.2 = ((bf16[128,8,2048]{2,1,0:T(8,128)(2,1)}), bf16[128,8,2048]{2,1,0:T(8,128)(2,1)}, u32[]{:S(2)}, u32[]{:S(2)}) async-start(bf16[128,8,2048]{2,1,0:T(8,128)(2,1)} %bitcast.37), calls=%async_computation.2 | async-start | bytes 8388608 | tf_op jit(solution)/shard_map/all_to_all | solution.py:527
  85.6 24.1 %expert_a.1 = (bf16[1024,1280]{1,0:T(8,128)(2,1)}, bf16[640,2048]{1,0:T(8,128)(2,1)}, bf16[640,2048]{1,0:T(8,128)(2,1)}, bf16[640,768]{1,0:T(8,128)(2,1)}, bf16[...) custom-call(bf16[1024,2560]{1,0:T(8,128)(2,1)} %bitcast.3.y_ref, bf16[2048,768]{1,0:T(8,128)(2,1)} %bitcast.44, ...), custom_call_target="tpu_custom_call" | custom-call | flops 10066329600 | bytes 40000000 | tf_op jit(solution)/shard_map/expert_a/pallas_call | solution.py:343
  109.7 7.5 %fusion.3 = f32[2048,768]{1,0:T(8,128)} fusion(bf16[640,2048]{1,0:T(8,128)(2,1)} %get-tuple-element.39, bf16[640,768]{1,0:T(8,128)(2,1)} %get-tuple-element.40), kind=kOutput, calls=%fused_computation.6 | convolution fusion | flops 2013265920 | bytes 9895936 | tf_op jit(solution)/shard_map/dot_general | solution.py:38
  117.1 0.0 copy-done.1
  117.1 0.0 copy-done.2
  117.1 4.6 %fusion.4 = f32[768,2048]{1,0:T(8,128)} fusion(bf16[640,768]{1,0:T(8,128)(2,1)S(1)} %copy-done.2, bf16[640,2048]{1,0:T(8,128)(2,1)S(1)} %copy-done.1), kind=kOutput, calls=%fused_computation.7 | convolution fusion | flops 2013265920 | bytes 9895936 | tf_op jit(solution)/shard_map/dot_general | solution.py:38
  121.8 13.9 %all-to-all-done.2 = bf16[128,8,2048]{2,1,0:T(8,128)(2,1)} async-done(((bf16[128,8,2048]{2,1,0:T(8,128)(2,1)}), bf16[128,8,2048]{2,1,0:T(8,128)(2,1)}, u32[]{:S(2)}, u32[]{:S(2)}) %all-to-all-start.2) | async-done | bytes 4194336 | tf_op jit(solution)/shard_map/all_to_all | solution.py:527
  135.6 7.2 %all-to-all-start.1 = ((bf16[128,8,1280]{2,1,0:T(8,128)(2,1)}), bf16[128,8,1280]{2,1,0:T(8,128)(2,1)S(1)}, u32[]{:S(2)}, u32[]{:S(2)}) async-start(bf16[128,8,1280]{2,1,0:T(8,128)(2,1)} %bitcast.38), calls=%async_computation.1 | async-start | bytes 5242880 | tf_op jit(solution)/shard_map/all_to_all | solution.py:527
  142.8 21.3 %expert_b.1 = (bf16[1024,1152]{1,0:T(8,128)(2,1)}, bf16[512,2048]{1,0:T(8,128)(2,1)}, bf16[512,2048]{1,0:T(8,128)(2,1)}, bf16[512,768]{1,0:T(8,128)(2,1)}, bf16[...) custom-call(bf16[1024,2048]{1,0:T(8,128)(2,1)} %bitcast.10.y_ref, bf16[2048,768]{1,0:T(8,128)(2,1)} %bitcast.46, ...), custom_call_target="tpu_custom_call" | custom-call | flops 8053063680 | bytes 40000000 | tf_op jit(solution)/shard_map/expert_b/pallas_call | solution.py:343
  164.1 11.7 %all-to-all-done.1 = bf16[128,8,1280]{2,1,0:T(8,128)(2,1)S(1)} async-done(((bf16[128,8,1280]{2,1,0:T(8,128)(2,1)}), bf16[128,8,1280]{2,1,0:T(8,128)(2,1)S(1)}, u32[]{:S(2)}, u32[]{:S(2)}) %all-to-all-start.1) | async-done | bytes 2621472 | tf_op jit(solution)/shard_map/all_to_all | solution.py:527
  175.8 8.7 %all-to-all-start.3 = ((bf16[128,8,1152]{2,1,0:T(8,128)(2,1)}), bf16[128,8,1152]{2,1,0:T(8,128)(2,1)}, u32[]{:S(2)}, u32[]{:S(2)}) async-start(bf16[128,8,1152]{2,1,0:T(8,128)(2,1)} %bitcast.39), calls=%async_computation.3 | async-start | bytes 4718592 | tf_op jit(solution)/shard_map/all_to_all | solution.py:527
  184.5 0.0 copy-start.3
  184.5 0.0 copy-start.6
  184.5 4.9 %fusion.5 = f32[2048,768]{1,0:T(8,128)S(1)} fusion(bf16[640,2048]{1,0:T(8,128)(2,1)} %get-tuple-element.39, bf16[640,768]{1,0:T(8,128)(2,1)} %get-tuple-element.52), kind=kOutput, calls=%fused_computation.8 | convolution fusion | flops 2013265920 | bytes 9895936 | tf_op jit(solution)/shard_map/dot_general | solution.py:38
  189.4 0.0 copy-done
  189.4 0.0 copy-done.3
  189.4 0.0 copy-done.6
  189.4 0.0 copy-start.5
  189.4 0.0 slice-start
  189.5 6.5 %fusion = bf16[1,2048,768]{2,1,0:T(8,128)(2,1)} fusion(f32[2048,768]{1,0:T(8,128)} %fusion.3, bf16[512,2048]{1,0:T(8,128)(2,1)S(1)} %copy-done.3, bf16[512,768]{1,0:T(8,128)(2,1)S(1)} %copy-done.6), kind=kOutput, calls=%fused_computation.3 | convolution fusion | flops 1613758464 | bytes 12320768 | tf_op jit(solution)/shard_map/dot_general | solution.py:38
  195.9 0.0 copy-done.5
  195.9 3.7 %fusion.1 = bf16[1,2048,768]{2,1,0:T(8,128)(2,1)} fusion(f32[2048,768]{1,0:T(8,128)S(1)} %fusion.5, bf16[512,2048]{1,0:T(8,128)(2,1)S(1)} %copy-done.3, bf16[512,768]{1,0:T(8,128)(2,1)S(1)} %copy-done.5), kind=kOutput, calls=%fused_computation.4 | convolution fusion | flops 1613758464 | bytes 12320768 | tf_op jit(solution)/shard_map/dot_general | solution.py:38
  199.7 0.0 slice-done
  199.7 0.0 slice-done.1
  199.7 3.7 %fusion.2 = bf16[1,768,2048]{2,1,0:T(8,128)(2,1)} fusion(f32[768,2048]{1,0:T(8,128)S(1)} %bitcast.35, bf16[512,768]{1,0:T(8,128)(2,1)S(1)} %copy-done.7, bf16[512,2048]{1,0:T(8,128)(2,1)S(1)} %copy-done.4), kind=kOutput, calls=%fused_computation.5 | convolution fusion | flops 1613758464 | bytes 12320768 | tf_op jit(solution)/shard_map/dot_general | solution.py:38
  203.4 3.7 %combine_a.1.part_hbm = f32[256,1024]{1,0:T(8,128)} custom-call(bf16[1024,256]{1,0:T(8,128)(2,1)} %get-tuple-element.36.sel_ref, bf16[128,128]{1,0:T(8,128)(2,1)} %get-tuple-element.34.sel9_ref.sel9_hbm, bf16[1024,1280]{1,0:T(8,128)(2,1)} %bitcast.32, bf16[1024,1280]{1,0:T(8,128)(2,1)} %bitcast.33), custom_call_target="tpu_custom_call" | custom-call | flops 536870912 | bytes 3670016 | tf_op jit(solution)/shard_map/combine_a/pallas_call | solution.py:404
  207.1 7.3 %all-to-all-done.3 = bf16[128,8,1152]{2,1,0:T(8,128)(2,1)} async-done(((bf16[128,8,1152]{2,1,0:T(8,128)(2,1)}), bf16[128,8,1152]{2,1,0:T(8,128)(2,1)}, u32[]{:S(2)}, u32[]{:S(2)}) %all-to-all-start.3) | async-done | bytes 2359328 | tf_op jit(solution)/shard_map/all_to_all | solution.py:527
  214.4 3.5 %combine_b.1 = (bf16[128,2048]{1,0:T(8,128)(2,1)}, bf16[8,128]{1,0:T(8,128)(2,1)}) custom-call(s32[8,128]{1,0:T(8,128)} %bitcast.41, bf16[8,128]{1,0:T(8,128)(2,1)} %bitcast.43, bf16[1024,128]{1,0:T(8,128)(2,1)} %get-tuple-element.33.mix_hbm, bf16[128,128]{1,0:T(8,128)(2,1)} %get-tuple-element.34.sel9_ref.sel9_hbm, ...), custom_call_target="tpu_custom_call" | custom-call | flops 536870912 | bytes 3407872 | tf_op jit(solution)/shard_map/combine_b/pallas_call | solution.py:498
  (9 shorter events, 0.0 us)
Async XLA Ops:
  4.9 72.6 %all-to-all-start = ((bf16[128,8,2560]{2,1,0:T(8,128)(2,1)}), bf16[128,8,2560]{2,1,0:T(8,128)(2,1)}, u32[]{:S(2)}, u32[]{:S(2)}) async-start(bf16[128,8,2560]{2,1,0:T(8,128)(2,1)} %bitcast.36), calls=%async_computation | async-start | bytes 10485760 | tf_op jit(solution)/shard_map/all_to_all | solution.py:527
  77.5 58.2 %all-to-all-start.2 = ((bf16[128,8,2048]{2,1,0:T(8,128)(2,1)}), bf16[128,8,2048]{2,1,0:T(8,128)(2,1)}, u32[]{:S(2)}, u32[]{:S(2)}) async-start(bf16[128,8,2048]{2,1,0:T(8,128)(2,1)} %bitcast.37), calls=%async_computation.2 | async-start | bytes 8388608 | tf_op jit(solution)/shard_map/all_to_all | solution.py:527
  109.7 7.5 %copy-start.1 = (bf16[640,2048]{1,0:T(8,128)(2,1)S(1)}, bf16[640,2048]{1,0:T(8,128)(2,1)}, u32[]{:S(2)}) copy-start(bf16[640,2048]{1,0:T(8,128)(2,1)} %get-tuple-element.42) | copy-start | bytes 7864324
  109.7 7.5 %copy-start.2 = (bf16[640,768]{1,0:T(8,128)(2,1)S(1)}, bf16[640,768]{1,0:T(8,128)(2,1)}, u32[]{:S(2)}) copy-start(bf16[640,768]{1,0:T(8,128)(2,1)} %get-tuple-element.41) | copy-start | bytes 2949124
  135.6 40.1 %all-to-all-start.1 = ((bf16[128,8,1280]{2,1,0:T(8,128)(2,1)}), bf16[128,8,1280]{2,1,0:T(8,128)(2,1)S(1)}, u32[]{:S(2)}, u32[]{:S(2)}) async-start(bf16[128,8,1280]{2,1,0:T(8,128)(2,1)} %bitcast.38), calls=%async_computation.1 | async-start | bytes 5242880 | tf_op jit(solution)/shard_map/all_to_all | solution.py:527
  175.8 13.6 %copy-start = (bf16[128,8,1280]{2,1,0:T(8,128)(2,1)}, bf16[128,8,1280]{2,1,0:T(8,128)(2,1)S(1)}, u32[]{:S(2)}) copy-start(bf16[128,8,1280]{2,1,0:T(8,128)(2,1)S(1)} %all-to-all-done.1) | copy-start | bytes 7864324
  175.8 38.6 %all-to-all-start.3 = ((bf16[128,8,1152]{2,1,0:T(8,128)(2,1)}), bf16[128,8,1152]{2,1,0:T(8,128)(2,1)}, u32[]{:S(2)}, u32[]{:S(2)}) async-start(bf16[128,8,1152]{2,1,0:T(8,128)(2,1)} %bitcast.39), calls=%async_computation.3 | async-start | bytes 4718592 | tf_op jit(solution)/shard_map/all_to_all | solution.py:527
  184.5 4.9 %copy-start.3 = (bf16[512,2048]{1,0:T(8,128)(2,1)S(1)}, bf16[512,2048]{1,0:T(8,128)(2,1)}, u32[]{:S(2)}) copy-start(bf16[512,2048]{1,0:T(8,128)(2,1)} %get-tuple-element.50) | copy-start | bytes 6291460
  184.5 4.9 %copy-start.6 = (bf16[512,768]{1,0:T(8,128)(2,1)S(1)}, bf16[512,768]{1,0:T(8,128)(2,1)}, u32[]{:S(2)}) copy-start(bf16[512,768]{1,0:T(8,128)(2,1)} %get-tuple-element.51) | copy-start | bytes 2359300
  189.4 6.5 %copy-start.5 = (bf16[512,768]{1,0:T(8,128)(2,1)S(1)}, bf16[512,768]{1,0:T(8,128)(2,1)}, u32[]{:S(2)}) copy-start(bf16[512,768]{1,0:T(8,128)(2,1)} %get-tuple-element.53) | copy-start | bytes 2359300
  189.4 10.2 %slice-start = ((s8[6291456]{0:T(1024)(128)(4,1)}), s8[4194304]{0:T(1024)(128)(4,1)S(1)}, s32[]{:S(2)}) async-start(s8[6291456]{0:T(1024)(128)(4,1)} %bitcast.34), calls=%async_computation.4 | async-start | bytes 8388608
  195.9 3.7 %slice-start.1 = ((s8[6291456]{0:T(1024)(128)(4,1)}), s8[2097152]{0:T(1024)(128)(4,1)S(1)}, s32[]{:S(2)}) async-start(s8[6291456]{0:T(1024)(128)(4,1)} %bitcast.34), calls=%async_computation.5 | async-start | bytes 4194304
  195.9 3.7 %copy-start.4 = (bf16[512,2048]{1,0:T(8,128)(2,1)S(1)}, bf16[512,2048]{1,0:T(8,128)(2,1)}, u32[]{:S(2)}) copy-start(bf16[512,2048]{1,0:T(8,128)(2,1)} %get-tuple-element.56) | copy-start | bytes 6291460
  195.9 3.7 %copy-start.7 = (bf16[512,768]{1,0:T(8,128)(2,1)S(1)}, bf16[512,768]{1,0:T(8,128)(2,1)}, u32[]{:S(2)}) copy-start(bf16[512,768]{1,0:T(8,128)(2,1)} %get-tuple-element.55) | copy-start | bytes 2359300

commit v4 on v3

--- a/solution.py
+++ b/solution.py
@@ -24,7 +24,8 @@
 FL = FOLD // LANE
 GROUP = 4 * E
 ROWS_A = GROUP + E
-SEND_A = 2 * HALF + 2 * FOLD
+ROWS_WIDE = 2 * HALF + 2 * FOLD
+SEND_A = ROWS_WIDE + LANE
 SEND_B = 2 * HALF
 BACK_A = HALF + FOLD
 BACK_B = HALF + LANE
@@ -68,10 +69,16 @@
     return jnp.concatenate([left, right], axis=1).astype(BF)
 
 
+def mix_rows(rank):
+    sub = lax.broadcasted_iota(jnp.int32, (E, SUB, T), 1)
+    slot = (sub // 2 + 4 * (sub % 2)).astype(F32)
+    return rank[:, None, :] == slot
+
+
 def pack_a_kernel(
-    ids_hbm, gates_hbm, x_hbm, g_hbm, out_hbm, sel_hbm, sel9_hbm, rank_hbm, gate_hbm,
-    ids_ref, gates_ref, x_ref, g_ref, sel_ref, sel9_ref, rank_ref, gate_ref,
-    selg, fold, out, in_sems, out_sems,
+    ids_hbm, gates_hbm, x_hbm, g_hbm, out_hbm, sel_hbm, sel9_hbm, rank_hbm,
+    ids_ref, gates_ref, x_ref, g_ref, sel_ref, sel9_ref, rank_ref,
+    fold, out, in_sems, out_sems,
 ):
     loads = [
         pltpu.make_async_copy(source, target, in_sems.at[n])
@@ -113,12 +120,9 @@
     rank = dot(member.astype(BF), earlier.astype(BF))
     rank = jnp.where(member > 0.0, rank, -1.0)
     rank_ref[...] = rank
-    gate_ref[...] = gate
     sel9 = jnp.where(rank == float(SUB), 1.0, 0.0)
     sel9_ref[...] = sel9.astype(BF)
-    sel9g = (sel9 * gate).astype(BF)
     sel_ref[...] = pair_select(rank, 1.0, 0)
-    selg[...] = pair_select(rank, gate[:, None, :], 0)
 
     tiles = HALF // TN
     loads[2].wait()
@@ -130,10 +134,10 @@
     loads[3].wait()
     for c in range(tiles):
         at = (tiles + 1 + c) * TN
-        out[:, at : at + TN] = dot(selg[...], halves(g_ref, c * TN, TN)).astype(BF)
+        out[:, at : at + TN] = dot(sel_ref[...], halves(g_ref, c * TN, TN)).astype(BF)
         send_piece(tiles + 1 + c)
     nine = dot(sel9_ref[...], x_ref[...])
-    nine_g = dot(sel9g, g_ref[...])
+    nine_g = dot(sel9_ref[...], g_ref[...])
     for i in range(SUB):
         rows = pl.ds(i, E, stride=SUB)
         for h in range(FL):
@@ -144,10 +148,18 @@
         at = HALF + h * LANE
         out[:, at : at + LANE] = fold[h].astype(BF)
     send_piece(tiles)
+    ones = jnp.ones((T, LANE), BF)
+    mixed = jnp.where(mix_rows(rank), gate[:, None, :], 0.0).reshape(R8, T)
+    own = dot(mixed.astype(BF), ones)
+    ninth = dot((sel9 * gate).astype(BF), ones)
+    ninth = jnp.broadcast_to(ninth[:, None, :], (E, SUB, LANE)).reshape(R8, LANE)
+    lane = lax.broadcasted_iota(jnp.int32, (R8, LANE), 1)
+    out[:, ROWS_WIDE:SEND_A] = jnp.where(lane == 1, ninth, own).astype(BF)
+    last = pl.ds(ROWS_WIDE, LANE)
+    send(out.at[:, last], out_hbm.at[:, last])
     send(sel_ref, sel_hbm)
     send(sel9_ref, sel9_hbm)
     send(rank_ref, rank_hbm)
-    send(gate_ref, gate_hbm)
     for store in stores:
         store.wait()
 
@@ -156,12 +168,11 @@
     return pl.pallas_call(
         pack_a_kernel,
         in_specs=[pl.BlockSpec(memory_space=pl.ANY)] * 4,
-        out_specs=[pl.BlockSpec(memory_space=pl.ANY)] * 5,
+        out_specs=[pl.BlockSpec(memory_space=pl.ANY)] * 4,
         out_shape=[
             jax.ShapeDtypeStruct((R8, SEND_A), BF),
             jax.ShapeDtypeStruct((R8, 2 * T), BF),
             jax.ShapeDtypeStruct((E, T), BF),
-            jax.ShapeDtypeStruct((E, T), F32),
             jax.ShapeDtypeStruct((E, T), F32),
         ],
         scratch_shapes=[
@@ -172,19 +183,17 @@
             pltpu.VMEM((R8, 2 * T), BF),
             pltpu.VMEM((E, T), BF),
             pltpu.VMEM((E, T), F32),
-            pltpu.VMEM((E, T), F32),
-            pltpu.VMEM((R8, 2 * T), BF),
             pltpu.VMEM((2 * FL, R8, LANE), F32),
             pltpu.VMEM((R8, SEND_A), BF),
             pltpu.SemaphoreType.DMA((4,)),
-            pltpu.SemaphoreType.DMA((SEND_A // TN + 4,)),
+            pltpu.SemaphoreType.DMA((ROWS_WIDE // TN + 5,)),
         ],
         cost_estimate=cost(4 * R8 * T * D, 2 * R8 * SEND_A + 4 * T * D),
         name="pack_a",
     )(ids_t, gates_t, acts, grad)
 
 
-def pack_b_kernel(rank_ref, gate_ref, x_ref, g_ref, out_ref, sel_t_ref, mix_ref, sel, selg):
+def pack_b_kernel(rank_ref, x_ref, g_ref, out_ref, sel_t_ref, mix_ref, sel):
     j = pl.program_id(0)
     tiles = HALF // TN
 
@@ -192,10 +201,7 @@
     def _():
         rank = rank_ref[...]
         sel[...] = pair_select(rank, 1.0, 4)
-        selg[...] = pair_select(rank, gate_ref[...][:, None, :], 4)
-        sub = lax.broadcasted_iota(jnp.int32, (E, SUB, T), 1)
-        slot = (sub // 2 + 4 * (sub % 2)).astype(F32)
-        mix_ref[...] = jnp.where(rank[:, None, :] == slot, 1.0, 0.0).reshape(R8, T).astype(BF)
+        mix_ref[...] = jnp.where(mix_rows(rank), 1.0, 0.0).reshape(R8, T).astype(BF)
 
     @pl.when(j == 1)
     def _():
@@ -209,17 +215,16 @@
 
         @pl.when(j == tiles + c)
         def _():
-            out_ref[...] = dot(selg[...], halves(g_ref, c * TN, TN)).astype(BF)
-
-
-def pack_b(rank, gate, acts, grad):
+            out_ref[...] = dot(sel[...], halves(g_ref, c * TN, TN)).astype(BF)
+
+
+def pack_b(rank, acts, grad):
     whole = lambda j: (0, 0)
     return pl.pallas_call(
         pack_b_kernel,
         grid=(SEND_B // TN,),
         in_specs=[
             pl.BlockSpec((E, T), whole),
-            pl.BlockSpec((E, T), whole),
             pl.BlockSpec((T, D), whole),
             pl.BlockSpec((T, D), whole),
         ],
@@ -233,20 +238,20 @@
             jax.ShapeDtypeStruct((2 * T, R8), BF),
             jax.ShapeDtypeStruct((R8, T), BF),
         ],
-        scratch_shapes=[pltpu.VMEM((R8, 2 * T), BF), pltpu.VMEM((R8, 2 * T), BF)],
+        scratch_shapes=[pltpu.VMEM((R8, 2 * T), BF)],
         compiler_params=ONE_DIM,
         cost_estimate=cost(4 * R8 * T * D, 2 * R8 * SEND_B + 4 * T * D),
         name="pack_b",
-    )(rank, gate, acts, grad)
+    )(rank, acts, grad)
 
 
 def expert_kernel(
-    nine, y_ref, wg_ref, wu_ref, wd_ref, wg2_ref, wu2_ref, *rest
+    nine, y_ref, gates_ref, wg_ref, wu_ref, wd_ref, wg2_ref, wu2_ref, *rest
 ):
     if nine:
-        out_ref, x_ref, g_ref, dpre_ref, dup_ref, hid_ref, tot_ref, fold, gsum = rest
+        out_ref, x_ref, g_ref, dpre_ref, dup_ref, hid_ref, tot_ref, fold, gsum, gcol = rest
     else:
-        tot_ref, out_ref, x_ref, g_ref, dpre_ref, dup_ref, hid_ref, fold, gsum = rest
+        tot_ref, out_ref, x_ref, g_ref, dpre_ref, dup_ref, hid_ref, fold, gsum, gcol = rest
     i = pl.program_id(0)
     rows_all = GROUP + (E if nine else 0)
     step = rows_all // 2
@@ -277,6 +282,12 @@
         unfold(0, HALF, x_ref)
         unfold(after, HALF + FOLD, g_ref)
         gsum[...] = jnp.zeros_like(gsum)
+        fold[0] = gates_ref[...].astype(F32)
+        own = fold[0, pl.ds(0 if nine else 1, GROUP, stride=2), :]
+        gcol[0:GROUP, :] = jnp.broadcast_to(own[:, 0:1], (GROUP, LANE))
+        if nine:
+            ninth = fold[0, pl.ds(0, E, stride=SUB), :]
+            gcol[GROUP:rows_all, :] = jnp.broadcast_to(ninth[:, 1:2], (E, LANE))
 
     @pl.when(i < N1)
     def _():
@@ -292,7 +303,9 @@
             hid = act * up
             part = hid * dh
             gsum[rows, :] += part[:, 0:LANE] + part[:, LANE:TF]
-            hid_ref[rows, cols] = hid.astype(BF)
+            gate = jnp.concatenate([gcol[rows, :]] * (TF // LANE), axis=1)
+            hid_ref[rows, cols] = (gate * hid).astype(BF)
+            dh = gate * dh
             dup_ref[rows, cols] = (dh * act).astype(BF)
             dpre_ref[rows, cols] = (dh * up * s * (1.0 + pre * (1.0 - s))).astype(BF)
 
@@ -334,7 +347,7 @@
             out_ref[:, lanes(HL)] = jnp.where(lane == 1, fold[1], fold[0]).astype(BF)
 
 
-def expert_side(nine, y, wg, wu, wd, *totals):
+def expert_side(nine, y, gates, wg, wu, wd, *totals):
     rows_all = GROUP + (E if nine else 0)
     send, back = (SEND_A, BACK_A) if nine else (SEND_B, BACK_B)
     first = lambda i: (0, jnp.minimum(i, N1 - 1))
@@ -344,7 +357,8 @@
         functools.partial(expert_kernel, nine),
         grid=(N1 + N2 + 1,),
         in_specs=[
-            pl.BlockSpec((R8, send), whole, pipeline_mode=SINGLE),
+            pl.BlockSpec((R8, ROWS_WIDE if nine else send), whole, pipeline_mode=SINGLE),
+            pl.BlockSpec((R8, LANE), lambda i: (0, ROWS_WIDE // LANE)),
             pl.BlockSpec((D, TF), first),
             pl.BlockSpec((D, TF), first),
             pl.BlockSpec((TF, D), lambda i: (jnp.minimum(i, N1 - 1), 0)),
@@ -373,11 +387,12 @@
         scratch_shapes=[
             pltpu.VMEM((HL + FL, R8, LANE), F32),
             pltpu.VMEM((rows_all, LANE), F32),
+            pltpu.VMEM((rows_all, LANE), F32),
         ],
         compiler_params=ONE_DIM,
         cost_estimate=cost(10 * rows_all * D * FF, 40e6),
         name="expert_a" if nine else "expert_b",
-    )(y, wg, wu, wd, wg, wu, *totals)
+    )(y, gates, wg, wu, wd, wg, wu, *totals)
 
 
 def combine_a_kernel(sel_ref, sel9_ref, y_ref, y9_ref, out_ref, fold, nine):
@@ -426,8 +441,8 @@
 
 
 def combine_b_kernel(
-    ids_hbm, gates_hbm, mix_hbm, sel9_hbm, sel_t_hbm, part_hbm, y_hbm, out_hbm, gg_hbm,
-    ids_ref, gates_ref, mix_ref, sel9_ref, sel_t_ref, part_ref, y_ref, out_ref, gg_ref,
+    ids_hbm, mix_hbm, sel9_hbm, sel_t_hbm, part_hbm, y_hbm, out_hbm, gg_hbm,
+    ids_ref, mix_ref, sel9_ref, sel_t_ref, part_ref, y_ref, out_ref, gg_ref,
     fold, in_sems, out_sems,
 ):
     pieces = HALF // CN
@@ -441,7 +456,6 @@
     gate_cols = pl.ds(HALF, LANE)
     small = [
         load(ids_hbm, ids_ref),
-        load(gates_hbm, gates_ref),
         load(sel9_hbm, sel9_ref),
         load(y_hbm.at[:, gate_cols], y_ref.at[:, gate_cols]),
         load(mix_hbm, mix_ref),
@@ -476,8 +490,7 @@
     for k in range(K):
         hit = ids_ref[k : k + 1, :] == expert
         totals.append(jnp.sum(jnp.where(hit, table, 0.0), axis=0, keepdims=True))
-    total = jnp.concatenate(totals, axis=0) / gates_ref[...].astype(F32)
-    gg_ref[...] = total.astype(BF)
+    gg_ref[...] = jnp.concatenate(totals, axis=0).astype(BF)
     send(gg_ref, gg_hbm)
     first.wait()
     for p in range(pieces):
@@ -494,10 +507,10 @@
         store.wait()
 
 
-def combine_b(ids_t, gates_t, mix, sel9, sel_t, part, y):
+def combine_b(ids_t, mix, sel9, sel_t, part, y):
     return pl.pallas_call(
         combine_b_kernel,
-        in_specs=[pl.BlockSpec(memory_space=pl.ANY)] * 7,
+        in_specs=[pl.BlockSpec(memory_space=pl.ANY)] * 6,
         out_specs=[pl.BlockSpec(memory_space=pl.ANY)] * 2,
         out_shape=[
             jax.ShapeDtypeStruct((T, D), BF),
@@ -505,7 +518,6 @@
         ],
         scratch_shapes=[
             pltpu.VMEM((K, T), jnp.int32),
-            pltpu.VMEM((K, T), BF),
             pltpu.VMEM((R8, T), BF),
             pltpu.VMEM((E, T), BF),
             pltpu.VMEM((2 * T, R8), BF),
@@ -519,7 +531,7 @@
         ],
         cost_estimate=cost(2 * R8 * T * D, 2 * R8 * BACK_B + 4 * T * D),
         name="combine_b",
-    )(ids_t, gates_t, mix, sel9, sel_t, part, y)
+    )(ids_t, mix, sel9, sel_t, part, y)
 
 
 def exchange(x):
@@ -534,22 +546,26 @@
     ids_t = expert_ids.T
     gates_t = gate_vals.T
     wg, wu, wd = w_gate[0], w_up[0], w_down[0]
-    send_a, sel_a, sel9, rank, gate = pack_a(ids_t, gates_t, acts, out_grad)
+    send_a, sel_a, sel9, rank = pack_a(ids_t, gates_t, acts, out_grad)
     got_a = exchange(send_a)
-    send_b, sel_b_t, mix = pack_b(rank, gate, acts, out_grad)
+    send_b, sel_b_t, mix = pack_b(rank, acts, out_grad)
     got_b = exchange(send_b)
-    back_a, x_a, g_a, dpre_a, dup_a, hid_a, totals = expert_side(True, got_a, wg, wu, wd)
+    back_a, x_a, g_a, dpre_a, dup_a, hid_a, totals = expert_side(
+        True, got_a, got_a, wg, wu, wd
+    )
     wg_part = dot(x_a, dpre_a, 0, 0)
     wd_part = dot(hid_a, g_a, 0, 0)
     back_a, wg_part, wd_part = lax.optimization_barrier((back_a, wg_part, wd_part))
     home_a = exchange(back_a)
-    back_b, x_b, g_b, dpre_b, dup_b, hid_b = expert_side(False, got_b, wg, wu, wd, totals)
+    back_b, x_b, g_b, dpre_b, dup_b, hid_b = expert_side(
+        False, got_b, got_a, wg, wu, wd, totals
+    )
     home_b = exchange(back_b)
     wg_grad = (wg_part + dot(x_b, dpre_b, 0, 0)).astype(BF)
     wu_grad = (dot(x_a, dup_a, 0, 0) + dot(x_b, dup_b, 0, 0)).astype(BF)
     wd_grad = (wd_part + dot(hid_b, g_b, 0, 0)).astype(BF)
     part = combine_a(sel_a, sel9, home_a)
-    grad_acts, gate_grad_t = combine_b(ids_t, gates_t, mix, sel9, sel_b_t, part, home_b)
+    grad_acts, gate_grad_t = combine_b(ids_t, mix, sel9, sel_b_t, part, home_b)
     return (
         grad_acts,
         gate_grad_t.T,

time: 222 us -> 225 us (1.014)
  waiting for transfers between devices: 88.8 us -> 94.3 us
  matrix products: 30.8 us -> 28.1 us
    all_to_all x4, waiting for transfers between devices: 88.8 us -> 94.3 us  [exchange(): lax.all_to_all(x.reshape(E, SUB, width), AXES, split_axis=0, concat_axis=...]
    dot_general x6, matrix products: 30.8 us -> 28.1 us  [dot(): lax.dot_general(a, b, (((ca,), (cb,)), ((), ())), preferred_element_type=...]
  transfers between devices with their start and end apart: 4 -> 4, of which waited for: 4 -> 4; matrix products, arithmetic and copies ran while one was open for 14% -> 13% of each run, Pallas kernels for 25% -> 25%
where the time goes in v4:
time: 225 us; the launch traced here: 221 us
  waiting for transfers between devices  94.3 us (42%)
  Pallas kernels  62.4 us (28%)
  starting transfers between devices  35.1 us (16%)
  matrix products  28.1 us (12%)
    all_to_all x4, waiting for transfers between devices, exchange(): lax.all_to_all(x.reshape(E, SUB, width), AXES, split_axis=0, concat_axis=...  94.3 us
    pallas_call x2, Pallas kernels, expert_side(): pl.pallas_call(functools.partial(expert_kernel, nine), grid=(N1 + N2 + 1,...  45.6 us
    all_to_all x4, starting transfers between devices, exchange(): lax.all_to_all(x.reshape(E, SUB, width), AXES, split_axis=0, concat_axis=...  35.1 us
    dot_general x6, matrix products, dot(): lax.dot_general(a, b, (((ca,), (cb,)), ((), ())), preferred_element_type=...  28.1 us
    pallas_call x1, Pallas kernels, pack_b(): pl.pallas_call(pack_b_kernel, grid=(SEND_B // TN,), in_specs=[pl.BlockSpe...  5.27 us
  transfers between devices with their start and end apart: 4, of which 4 were waited for; matrix products, arithmetic and copies ran while one was open for 13% of the time, Pallas kernels for 25%

profile of v4, /device:TPU:13, one launch (start us, length us, event | category | flops | bytes accessed | tf_op | source)
XLA Modules:
  0.0 221.0 jit_solution(2605548497867935438)
XLA Ops:
  0.6 4.4 %pack_a.1 = (bf16[1024,2688]{1,0:T(8,128)(2,1)}, bf16[1024,256]{1,0:T(8,128)(2,1)}, bf16[128,128]{1,0:T(8,128)(2,1)}, f32[128,128]{1,0:T(8,128)}) custom-call(s32[8,128]{1,0:T(8,128)} %bitcast.40, bf16[8,128]{1,0:T(8,128)(2,1)} %bitcast.52, bf16[128,2048]{1,0:T(8,128)(2,1)} %x_ref.1, bf16[128,2048]{1,0:T(8,128)(2,1)} %g_ref.1), custom_call_target="tpu_custom_call" | custom-call | flops 1073741824 | bytes 6553600 | tf_op jit(solution)/shard_map/pack_a/pallas_call | solution.py:168
  5.0 11.1 %all-to-all-start = ((bf16[128,8,2688]{2,1,0:T(8,128)(2,1)}), bf16[128,8,2688]{2,1,0:T(8,128)(2,1)}, u32[]{:S(2)}, u32[]{:S(2)}) async-start(bf16[128,8,2688]{2,1,0:T(8,128)(2,1)} %bitcast.36), calls=%async_computation | async-start | bytes 11010048 | tf_op jit(solution)/shard_map/all_to_all | solution.py:539
  16.1 5.3 %pack_b.1 = (bf16[1024,2048]{1,0:T(8,128)(2,1)}, bf16[256,1024]{1,0:T(8,128)(2,1)}, bf16[1024,128]{1,0:T(8,128)(2,1)}) custom-call(f32[128,128]{1,0:T(8,128)} %get-tuple-element.30.rank_ref, bf16[128,2048]{1,0:T(8,128)(2,1)} %x_ref.1, bf16[128,2048]{1,0:T(8,128)(2,1)} %g_ref.1), custom_call_target="tpu_custom_call" | custom-call | flops 1073741824 | bytes 5242880 | tf_op jit(solution)/shard_map/pack_b/pallas_call | solution.py:223
  21.4 59.1 %all-to-all-done = bf16[128,8,2688]{2,1,0:T(8,128)(2,1)} async-done(((bf16[128,8,2688]{2,1,0:T(8,128)(2,1)}), bf16[128,8,2688]{2,1,0:T(8,128)(2,1)}, u32[]{:S(2)}, u32[]{:S(2)}) %all-to-all-start) | async-done | bytes 5505056 | tf_op jit(solution)/shard_map/all_to_all | solution.py:539
  80.5 8.1 %all-to-all-start.2 = ((bf16[128,8,2048]{2,1,0:T(8,128)(2,1)}), bf16[128,8,2048]{2,1,0:T(8,128)(2,1)}, u32[]{:S(2)}, u32[]{:S(2)}) async-start(bf16[128,8,2048]{2,1,0:T(8,128)(2,1)} %bitcast.37), calls=%async_computation.2 | async-start | bytes 8388608 | tf_op jit(solution)/shard_map/all_to_all | solution.py:539
  88.6 24.2 %expert_a.1 = (bf16[1024,1280]{1,0:T(8,128)(2,1)}, bf16[640,2048]{1,0:T(8,128)(2,1)}, bf16[640,2048]{1,0:T(8,128)(2,1)}, bf16[640,768]{1,0:T(8,128)(2,1)}, bf16[...) custom-call(bf16[1024,2688]{1,0:T(8,128)(2,1)} %bitcast.3.y_ref.gates_ref, ...), custom_call_target="tpu_custom_call" | custom-call | flops 10066329600 | bytes 40000000 | tf_op jit(solution)/shard_map/expert_a/pallas_call | solution.py:356
  112.8 7.5 %fusion.3 = f32[2048,768]{1,0:T(8,128)} fusion(bf16[640,2048]{1,0:T(8,128)(2,1)} %get-tuple-element.37, bf16[640,768]{1,0:T(8,128)(2,1)} %get-tuple-element.38), kind=kOutput, calls=%fused_computation.6 | convolution fusion | flops 2013265920 | bytes 9895936 | tf_op jit(solution)/shard_map/dot_general | solution.py:39
  120.2 0.0 copy-done.1
  120.2 0.0 copy-done.2
  120.2 4.6 %fusion.4 = f32[768,2048]{1,0:T(8,128)} fusion(bf16[640,768]{1,0:T(8,128)(2,1)S(1)} %copy-done.2, bf16[640,2048]{1,0:T(8,128)(2,1)S(1)} %copy-done.1), kind=kOutput, calls=%fused_computation.7 | convolution fusion | flops 2013265920 | bytes 9895936 | tf_op jit(solution)/shard_map/dot_general | solution.py:39
  124.9 13.7 %all-to-all-done.2 = bf16[128,8,2048]{2,1,0:T(8,128)(2,1)} async-done(((bf16[128,8,2048]{2,1,0:T(8,128)(2,1)}), bf16[128,8,2048]{2,1,0:T(8,128)(2,1)}, u32[]{:S(2)}, u32[]{:S(2)}) %all-to-all-start.2) | async-done | bytes 4194336 | tf_op jit(solution)/shard_map/all_to_all | solution.py:539
  138.6 7.2 %all-to-all-start.1 = ((bf16[128,8,1280]{2,1,0:T(8,128)(2,1)}), bf16[128,8,1280]{2,1,0:T(8,128)(2,1)S(1)}, u32[]{:S(2)}, u32[]{:S(2)}) async-start(bf16[128,8,1280]{2,1,0:T(8,128)(2,1)} %bitcast.38), calls=%async_computation.1 | async-start | bytes 5242880 | tf_op jit(solution)/shard_map/all_to_all | solution.py:539
  145.8 21.4 %expert_b.1 = (bf16[1024,1152]{1,0:T(8,128)(2,1)}, bf16[512,2048]{1,0:T(8,128)(2,1)}, bf16[512,2048]{1,0:T(8,128)(2,1)}, bf16[512,768]{1,0:T(8,128)(2,1)}, bf16[...) custom-call(bf16[1024,2048]{1,0:T(8,128)(2,1)} %bitcast.10.y_ref, bf16[1024,2688]{1,0:T(8,128)(2,1)} %bitcast.3.y_ref.gates_ref, ...), custom_call_target="tpu_custom_call" | custom-call | flops 8053063680 | bytes 40000000 | tf_op jit(solution)/shard_map/expert_b/pallas_call | solution.py:356
  167.1 11.6 %all-to-all-done.1 = bf16[128,8,1280]{2,1,0:T(8,128)(2,1)S(1)} async-done(((bf16[128,8,1280]{2,1,0:T(8,128)(2,1)}), bf16[128,8,1280]{2,1,0:T(8,128)(2,1)S(1)}, u32[]{:S(2)}, u32[]{:S(2)}) %all-to-all-start.1) | async-done | bytes 2621472 | tf_op jit(solution)/shard_map/all_to_all | solution.py:539
  178.7 8.7 %all-to-all-start.3 = ((bf16[128,8,1152]{2,1,0:T(8,128)(2,1)}), bf16[128,8,1152]{2,1,0:T(8,128)(2,1)}, u32[]{:S(2)}, u32[]{:S(2)}) async-start(bf16[128,8,1152]{2,1,0:T(8,128)(2,1)} %bitcast.39), calls=%async_computation.3 | async-start | bytes 4718592 | tf_op jit(solution)/shard_map/all_to_all | solution.py:539
  187.5 0.0 copy-start.3
  187.5 0.0 copy-start.6
  187.5 0.0 slice-start.2
  187.5 4.9 %fusion.5 = f32[2048,768]{1,0:T(8,128)S(1)} fusion(bf16[640,2048]{1,0:T(8,128)(2,1)} %get-tuple-element.37, bf16[640,768]{1,0:T(8,128)(2,1)} %get-tuple-element.50), kind=kOutput, calls=%fused_computation.8 | convolution fusion | flops 2013265920 | bytes 9895936 | tf_op jit(solution)/shard_map/dot_general | solution.py:39
  192.3 0.0 copy-done
  192.4 0.0 copy-done.3
  192.4 0.0 copy-done.6
  192.4 0.0 slice-start.3
  192.4 0.0 slice-start
  192.4 3.7 %fusion.1 = bf16[1,2048,768]{2,1,0:T(8,128)(2,1)} fusion(f32[2048,768]{1,0:T(8,128)S(1)} %fusion.5, bf16[512,2048]{1,0:T(8,128)(2,1)S(1)} %copy-done.3, bf16[512,768]{1,0:T(8,128)(2,1)S(1)} %copy-done.6), kind=kOutput, calls=%fused_computation.4 | convolution fusion | flops 1613758464 | bytes 12320768 | tf_op jit(solution)/shard_map/dot_general | solution.py:39
  196.1 0.0 slice-start.1
  196.2 3.7 %fusion = bf16[1,2048,768]{2,1,0:T(8,128)(2,1)} fusion(f32[2048,768]{1,0:T(8,128)S(1)} %bitcast.55, bf16[512,2048]{1,0:T(8,128)(2,1)S(1)} %copy-done.3, bf16[512,768]{1,0:T(8,128)(2,1)S(1)} %copy-done.5), kind=kOutput, calls=%fused_computation.3 | convolution fusion | flops 1613758464 | bytes 12320768 | tf_op jit(solution)/shard_map/dot_general | solution.py:39
  199.9 0.0 slice-done.1
  199.9 3.7 %fusion.2 = bf16[1,768,2048]{2,1,0:T(8,128)(2,1)} fusion(f32[768,2048]{1,0:T(8,128)S(1)} %bitcast.35, bf16[512,768]{1,0:T(8,128)(2,1)S(1)} %copy-done.7, bf16[512,2048]{1,0:T(8,128)(2,1)S(1)} %copy-done.4), kind=kOutput, calls=%fused_computation.5 | convolution fusion | flops 1613758464 | bytes 12320768 | tf_op jit(solution)/shard_map/dot_general | solution.py:39
  203.6 3.7 %combine_a.1.part_hbm = f32[256,1024]{1,0:T(8,128)} custom-call(bf16[1024,256]{1,0:T(8,128)(2,1)} %get-tuple-element.34.sel_ref, bf16[128,128]{1,0:T(8,128)(2,1)} %get-tuple-element.32.sel9_ref.sel9_hbm, bf16[1024,1280]{1,0:T(8,128)(2,1)} %bitcast.32, bf16[1024,1280]{1,0:T(8,128)(2,1)} %bitcast.33), custom_call_target="tpu_custom_call" | custom-call | flops 536870912 | bytes 3670016 | tf_op jit(solution)/shard_map/combine_a/pallas_call | solution.py:419
  207.3 10.0 %all-to-all-done.3 = bf16[128,8,1152]{2,1,0:T(8,128)(2,1)} async-done(((bf16[128,8,1152]{2,1,0:T(8,128)(2,1)}), bf16[128,8,1152]{2,1,0:T(8,128)(2,1)}, u32[]{:S(2)}, u32[]{:S(2)}) %all-to-all-start.3) | async-done | bytes 2359328 | tf_op jit(solution)/shard_map/all_to_all | solution.py:539
  217.3 3.5 %combine_b.1 = (bf16[128,2048]{1,0:T(8,128)(2,1)}, bf16[8,128]{1,0:T(8,128)(2,1)}) custom-call(s32[8,128]{1,0:T(8,128)} %bitcast.41, bf16[1024,128]{1,0:T(8,128)(2,1)} %get-tuple-element.31.mix_hbm, bf16[128,128]{1,0:T(8,128)(2,1)} %get-tuple-element.32.sel9_ref.sel9_hbm, bf16[256,1024]{1,0:T(8,128)(2,1)} %get-tuple-element.33.sel_t_hbm, ...), custom_call_target="tpu_custom_call" | custom-call | flops 536870912 | bytes 3407872 | tf_op jit(solution)/shard_map/combine_b/pallas_call | solution.py:511
  (14 shorter events, 0.0 us)
Async XLA Ops:
  5.0 75.4 %all-to-all-start = ((bf16[128,8,2688]{2,1,0:T(8,128)(2,1)}), bf16[128,8,2688]{2,1,0:T(8,128)(2,1)}, u32[]{:S(2)}, u32[]{:S(2)}) async-start(bf16[128,8,2688]{2,1,0:T(8,128)(2,1)} %bitcast.36), calls=%async_computation | async-start | bytes 11010048 | tf_op jit(solution)/shard_map/all_to_all | solution.py:539
  80.5 58.1 %all-to-all-start.2 = ((bf16[128,8,2048]{2,1,0:T(8,128)(2,1)}), bf16[128,8,2048]{2,1,0:T(8,128)(2,1)}, u32[]{:S(2)}, u32[]{:S(2)}) async-start(bf16[128,8,2048]{2,1,0:T(8,128)(2,1)} %bitcast.37), calls=%async_computation.2 | async-start | bytes 8388608 | tf_op jit(solution)/shard_map/all_to_all | solution.py:539
  112.8 7.5 %copy-start.1 = (bf16[640,2048]{1,0:T(8,128)(2,1)S(1)}, bf16[640,2048]{1,0:T(8,128)(2,1)}, u32[]{:S(2)}) copy-start(bf16[640,2048]{1,0:T(8,128)(2,1)} %get-tuple-element.40) | copy-start | bytes 7864324
  112.8 7.5 %copy-start.2 = (bf16[640,768]{1,0:T(8,128)(2,1)S(1)}, bf16[640,768]{1,0:T(8,128)(2,1)}, u32[]{:S(2)}) copy-start(bf16[640,768]{1,0:T(8,128)(2,1)} %get-tuple-element.39) | copy-start | bytes 2949124
  138.6 40.1 %all-to-all-start.1 = ((bf16[128,8,1280]{2,1,0:T(8,128)(2,1)}), bf16[128,8,1280]{2,1,0:T(8,128)(2,1)S(1)}, u32[]{:S(2)}, u32[]{:S(2)}) async-start(bf16[128,8,1280]{2,1,0:T(8,128)(2,1)} %bitcast.38), calls=%async_computation.1 | async-start | bytes 5242880 | tf_op jit(solution)/shard_map/all_to_all | solution.py:539
  178.7 13.6 %copy-start = (bf16[128,8,1280]{2,1,0:T(8,128)(2,1)}, bf16[128,8,1280]{2,1,0:T(8,128)(2,1)S(1)}, u32[]{:S(2)}) copy-start(bf16[128,8,1280]{2,1,0:T(8,128)(2,1)S(1)} %all-to-all-done.1) | copy-start | bytes 7864324
  178.7 38.6 %all-to-all-start.3 = ((bf16[128,8,1152]{2,1,0:T(8,128)(2,1)}), bf16[128,8,1152]{2,1,0:T(8,128)(2,1)}, u32[]{:S(2)}, u32[]{:S(2)}) async-start(bf16[128,8,1152]{2,1,0:T(8,128)(2,1)} %bitcast.39), calls=%async_computation.3 | async-start | bytes 4718592 | tf_op jit(solution)/shard_map/all_to_all | solution.py:539
  187.5 4.9 %copy-start.3 = (bf16[512,2048]{1,0:T(8,128)(2,1)S(1)}, bf16[512,2048]{1,0:T(8,128)(2,1)}, u32[]{:S(2)}) copy-start(bf16[512,2048]{1,0:T(8,128)(2,1)} %get-tuple-element.48) | copy-start | bytes 6291460
  187.5 4.9 %copy-start.6 = (bf16[512,768]{1,0:T(8,128)(2,1)S(1)}, bf16[512,768]{1,0:T(8,128)(2,1)}, u32[]{:S(2)}) copy-start(bf16[512,768]{1,0:T(8,128)(2,1)} %get-tuple-element.51) | copy-start | bytes 2359300
  187.5 8.7 %slice-start.2 = ((s8[6291456]{0:T(1024)(128)(4,1)}), s8[4194304]{0:T(1024)(128)(4,1)S(1)}, s32[]{:S(2)}) async-start(s8[6291456]{0:T(1024)(128)(4,1)} %bitcast.54), calls=%async_computation.6 | async-start | bytes 8388608
  192.4 3.8 %slice-start.3 = ((s8[6291456]{0:T(1024)(128)(4,1)}), s8[2097152]{0:T(1024)(128)(4,1)S(1)}, s32[]{:S(2)}) async-start(s8[6291456]{0:T(1024)(128)(4,1)} %bitcast.54), calls=%async_computation.7 | async-start | bytes 4194304
  192.4 3.7 %copy-start.5 = (bf16[512,768]{1,0:T(8,128)(2,1)S(1)}, bf16[512,768]{1,0:T(8,128)(2,1)}, u32[]{:S(2)}) copy-start(bf16[512,768]{1,0:T(8,128)(2,1)} %get-tuple-element.49) | copy-start | bytes 2359300
  192.4 7.5 %slice-start = ((s8[6291456]{0:T(1024)(128)(4,1)}), s8[4194304]{0:T(1024)(128)(4,1)S(1)}, s32[]{:S(2)}) async-start(s8[6291456]{0:T(1024)(128)(4,1)} %bitcast.34), calls=%async_computation.4 | async-start | bytes 8388608
  196.1 3.8 %slice-start.1 = ((s8[6291456]{0:T(1024)(128)(4,1)}), s8[2097152]{0:T(1024)(128)(4,1)S(1)}, s32[]{:S(2)}) async-start(s8[6291456]{0:T(1024)(128)(4,1)} %bitcast.34), calls=%async_computation.5 | async-start | bytes 4194304
  196.1 3.7 %copy-start.4 = (bf16[512,2048]{1,0:T(8,128)(2,1)S(1)}, bf16[512,2048]{1,0:T(8,128)(2,1)}, u32[]{:S(2)}) copy-start(bf16[512,2048]{1,0:T(8,128)(2,1)} %get-tuple-element.54) | copy-start | bytes 6291460
  196.2 3.7 %copy-start.7 = (bf16[512,768]{1,0:T(8,128)(2,1)S(1)}, bf16[512,768]{1,0:T(8,128)(2,1)}, u32[]{:S(2)}) copy-start(bf16[512,768]{1,0:T(8,128)(2,1)} %get-tuple-element.53) | copy-start | bytes 2359300
